TPU v7x, 256 devices: a whole 4x4x8 slice. The times are simulated.
256 devices in a mesh: frames: 8 (over z_lo, y), slab: 32 (over z_hi, x, core).
Axes of the slice: x: 4, y: 4, z: 8 (z_hi: 4, z_lo: 2; z = z_hi * 2 + z_lo), core: 2. Of those that a mesh axis runs over, the one named last changes fastest.
Arguments:
- raw_movie: bfloat16 [16, 2048, 128], P('frames', 'slab'), may hold values from -18 to 18
- shifts: int32 [2, 16, 64, 1], P(None, 'frames', 'slab'), may hold values from -3 to 3
- footprints: bfloat16 [1024, 16, 16], P('slab'), may hold values from 0.049804688 to 1
- anchors: int32 [1024, 2], P('slab'), may hold values from 0 to 2032, as said below
- block_of: int32 [1024], P('slab'), may hold values from 0 to 3, as said below
- init_traces: float32 [1024, 16], P('slab', 'frames'), may hold values from -6 to 6
Outputs:
- traces_z: float32 [1024, 16], P('slab', 'frames')
- residual: float32 [16, 2048, 128], P('frames', 'slab')
Inputs may be any that keep to these rules, and one draw needn't show every extreme that they name: `anchors`: the tile of a source owned by slab s (sources s * 32 to s * 32 + 31) has its top row in s * 64 - 16 // 2 to s * 64 + 64 - 16 // 2 - 1, moved into the grid where it would leave it; its left column lies in 0 to 112. `block_of`: among the 32 sources of one slab, each block number is held by at most 16 sources, and some block number by exactly 16.
All inputs are finite; a program needn't handle non-finite values.
Results may differ from a plain program's by a relative error of at most 0.003.
Values may be sent and summed in bfloat16 or wider, within the bound.
A program may use at most 64 MiB of HBM per device.

v0:
```python
import jax
import jax.numpy as jnp
from jax import lax
from jax.sharding import PartitionSpec as P

SHIFT = 3
PATCH_R = 32
PATCH_C = 128
BLOCKS = 4
SWEEPS = 3


WEIGHT_NEAR = 0.75
WEIGHT_FAR = 0.25
EPSILON = 1e-05
HIGHEST = lax.Precision.HIGHEST


def extended(block, sides, width):
    for axis, dim in sides:
        count = lax.axis_size(axis)
        forward = [(i, i + 1) for i in range(count - 1)]
        backward = [(target, source) for source, target in forward]
        low = lax.ppermute(
            lax.slice_in_dim(block, block.shape[dim] - width, None, axis=dim), axis, forward
        )
        high = lax.ppermute(lax.slice_in_dim(block, 0, width, axis=dim), axis, backward)
        block = jnp.concatenate([low, block, high], axis=dim)
    return block


def warp_frame(padded, rows_shift, cols_shift):
    count_r, count_c = rows_shift.shape

    def one_patch(patch_row, patch_col, row_shift, col_shift):
        window = lax.dynamic_slice(
            padded,
            (SHIFT + 1 + patch_row * PATCH_R + row_shift, SHIFT + patch_col * PATCH_C + col_shift),
            (PATCH_R + 1, PATCH_C),
        ).astype(jnp.float32)
        return WEIGHT_NEAR * window[:-1] + WEIGHT_FAR * window[1:]

    across = jax.vmap(one_patch, in_axes=(None, 0, 0, 0))
    layout = jax.vmap(across, in_axes=(0, None, 0, 0))(
        jnp.arange(count_r, dtype=jnp.int32),
        jnp.arange(count_c, dtype=jnp.int32),
        rows_shift,
        cols_shift,
    )
    return layout.transpose(0, 2, 1, 3).reshape(count_r * PATCH_R, count_c * PATCH_C)


def place_cols(tiles, col_anchor, col_count):
    tile_size = tiles.shape[1]
    offsets = jnp.arange(tile_size, dtype=jnp.int32)
    places = jnp.arange(col_count, dtype=jnp.int32)
    onehot = (col_anchor[:, None, None] + offsets[None, :, None] == places[None, None, :]).astype(
        jnp.float32
    )
    placed = jnp.einsum("kij,kjx->kix", tiles, onehot, precision=HIGHEST)
    return placed.reshape(-1, col_count)


def place_rows(row_anchor, base_row, tile_size, ext_rows):
    offsets = jnp.arange(tile_size, dtype=jnp.int32)
    position = (row_anchor - base_row)[:, None] + offsets[None, :]
    places = jnp.arange(ext_rows, dtype=jnp.int32)
    return (places[:, None] == position.reshape(-1)[None, :]).astype(jnp.float32)


def render_with(values, col_placed, row_onehot, tile_size):
    repeated = jnp.repeat(values.T, tile_size, axis=1)
    mixed = row_onehot[None] * repeated[:, None, :]
    return jnp.einsum("tyr,rx->tyx", mixed, col_placed, precision=HIGHEST)


def project_with(residual, col_placed, row_onehot, tile_size):
    partial_rows = jnp.einsum("tyx,rx->tyr", residual, col_placed, precision=HIGHEST)
    picked = jnp.sum(partial_rows * row_onehot[None], axis=1)
    frame_count = picked.shape[0]
    return picked.reshape(frame_count, -1, tile_size).sum(axis=2).T


def shards(raw_movie, shifts, footprints, anchors, block_of, init_traces):
    frame_count = raw_movie.shape[0]
    slab_rows = raw_movie.shape[1]
    col_count = raw_movie.shape[2]
    tile_size = footprints.shape[1]
    rim_rows = tile_size // 2
    ext_rows = slab_rows + 2 * rim_rows
    slab_index = lax.axis_index("slab")
    widened = extended(raw_movie, (("slab", 1),), SHIFT + 1)
    padded = jnp.pad(widened, ((0, 0), (0, 0), (SHIFT, SHIFT)))
    corrected = jax.vmap(warp_frame)(padded, shifts[0], shifts[1]).astype(jnp.bfloat16)
    movie_ext = extended(corrected, (("slab", 1),), rim_rows)
    weights = footprints.astype(jnp.float32)
    norm_sq = jnp.sum(weights * weights, axis=(1, 2))
    base_row = slab_index * slab_rows - rim_rows
    own_cols = place_cols(weights, anchors[:, 1], col_count)
    own_rows = place_rows(anchors[:, 0], base_row, tile_size, ext_rows)

    def total_change(sel_cols, sel_rows, sel_change):
        change_img = render_with(sel_change, sel_cols, sel_rows, tile_size)
        widened_change = extended(change_img, (("slab", 1),), 2 * rim_rows)
        from_above = widened_change[:, : 2 * rim_rows]
        from_below = widened_change[:, widened_change.shape[1] - 2 * rim_rows :]
        rim_terms = jnp.pad(from_above, ((0, 0), (0, ext_rows - 2 * rim_rows), (0, 0))) + jnp.pad(
            from_below, ((0, 0), (ext_rows - 2 * rim_rows, 0), (0, 0))
        )
        return change_img + rim_terms

    residual_ext = movie_ext.astype(jnp.float32) - total_change(own_cols, own_rows, init_traces)
    traces = init_traces
    for sweep_idx in range(SWEEPS):
        for block_idx in range(BLOCKS):
            in_block = block_of == block_idx
            sel_cols, sel_rows = (own_cols, own_rows)
            projected = project_with(residual_ext, own_cols, own_rows, tile_size)
            full_change = jnp.where(
                in_block[:, None], projected / norm_sq[:, None], jnp.zeros_like(projected)
            )
            sel_change = full_change
            traces = traces + full_change
            residual_ext = residual_ext - total_change(sel_cols, sel_rows, sel_change)
    moments = lax.psum((jnp.sum(traces, axis=1), jnp.sum(traces * traces, axis=1)), "frames")
    frame_total = frame_count * lax.axis_size("frames")
    trace_mean = (moments[0] / frame_total)[:, None]
    square_mean = (moments[1] / frame_total)[:, None]
    spread = square_mean - trace_mean * trace_mean
    traces_z = (traces - trace_mean) / jnp.sqrt(spread + EPSILON)
    return (traces_z, residual_ext[:, rim_rows : rim_rows + slab_rows])


def solution(mesh):
    in_specs = (
        P("frames", "slab", None),
        P(None, "frames", "slab", None),
        P("slab", None, None),
        P("slab", None),
        P("slab"),
        P("slab", "frames"),
    )
    out_specs = (P("slab", "frames"), P("frames", "slab", None))
    return jax.shard_map(shards, mesh=mesh, in_specs=in_specs, out_specs=out_specs, check_vma=False)
```

profile of v0, /device:TPU:128, one launch (start us, length us, event | category | flops | bytes accessed | tf_op | source)
XLA Modules:
  0.0 214.6 jit_solution(16632131391023334139)
XLA Ops:
  0.6 0.7 fusion.96
  1.3 1.9 collective-permute-start
  3.3 7.9 %collective-permute-start.1 = (bf16[2,4,128]{2,1,0:T(4,128)(2,1)S(1)}, bf16[2,4,128]{2,1,0:T(4,128)(2,1)S(1)}, u32[]{:S(2)}, u32[]{:S(2)}) collective-permute-start(bf16[2,4,128]{2,1,0:T(4,128)(2,1)S(1)} %get-tuple-element.56), channel_id=1, source_target_pairs={{1,0},{2,1},{3,2},{4,3},{5,4},{6,5},{7,6},{8,7},{9,8},{10,9},{11,1... | collective-permute-start | bytes 6152 | tf_op jit(solution)/shard_map/ppermute | solution.py:27
  11.1 0.7 copy-done.4
  12.0 0.5 copy-done.2
  13.6 1.9 collective-permute-start.4
  15.5 7.9 %collective-permute-start.5 = (f32[2,16,128]{2,1,0:T(8,128)S(1)}, f32[2,16,128]{2,1,0:T(8,128)S(1)}, u32[]{:S(2)}, u32[]{:S(2)}) collective-permute-start(f32[2,16,128]{2,1,0:T(8,128)S(1)} %get-tuple-element.52), channel_id=1, source_target_pairs={{1,0},{2,1},{3,2},{4,3},{5,4},{6,5},{7,6},{8,7},{9,8},{10,9},{11,1... | collective-permute-start | bytes 49160 | tf_op jit(solution)/shard_map/ppermute | solution.py:27
  23.7 10.7 %while.1 = (s32[]{:T(128)}, bf16[2,72,134]{2,1,0:T(8,128)(2,1)S(1)}, s32[4,3]{1,0:T(4,128)S(1)}, bf16[4,33,128]{2,1,0:T(8,128)(2,1)S(1)}, s32[]{:T(128)}) while((s32[]{:T(128)}, bf16[2,72,134]{2,1,0:T(8,128)(2,1)S(1)}, s32[4,3]{1,0:T(4,128)S(1)}, bf16[4,33,128]{2,1,0:T(8,128)(2,1)S(1)}, s32[]{:T(128)}) %tuple.54), condition=%wide.while_cond, body=%wide.while_body.sunk | while | flops 2 | bytes 20617 | solution.py:36
  23.8 0.7 fusion.131
  24.4 2.0 dynamic-slice_dynamic-update-slice_fusion.2
  26.4 0.7 fusion.131
  27.1 2.0 dynamic-slice_dynamic-update-slice_fusion.2
  29.1 0.7 fusion.131
  29.8 2.0 dynamic-slice_dynamic-update-slice_fusion.2
  31.8 0.7 fusion.131
  32.4 2.0 dynamic-slice_dynamic-update-slice_fusion.2
  34.5 1.9 collective-permute-start.2
  36.4 7.9 %collective-permute-start.3 = (bf16[2,8,128]{2,1,0:T(8,128)(2,1)S(1)}, bf16[2,8,128]{2,1,0:T(8,128)(2,1)S(1)}, u32[]{:S(2)}, u32[]{:S(2)}) collective-permute-start(bf16[2,8,128]{2,1,0:T(8,128)(2,1)S(1)} %get-tuple-element.54), channel_id=1, source_target_pairs={{1,0},{2,1},{3,2},{4,3},{5,4},{6,5},{7,6},{8,7},{9,8},{10,9},{11,1... | collective-permute-start | bytes 12296 | tf_op jit(solution)/shard_map/ppermute | solution.py:27
  44.3 1.3 collective-permute-done.3
  45.6 0.4 fusion
  46.8 1.9 collective-permute-start.6
  48.8 7.9 %collective-permute-start.7 = (f32[2,16,128]{2,1,0:T(8,128)S(1)}, f32[2,16,128]{2,1,0:T(8,128)S(1)}, u32[]{:S(2)}, u32[]{:S(2)}) collective-permute-start(f32[2,16,128]{2,1,0:T(8,128)S(1)} %get-tuple-element.50), channel_id=1, source_target_pairs={{1,0},{2,1},{3,2},{4,3},{5,4},{6,5},{7,6},{8,7},{9,8},{10,9},{11,1... | collective-permute-start | bytes 49160 | tf_op jit(solution)/shard_map/ppermute | solution.py:27
  56.6 1.4 collective-permute-done.7
  59.3 1.9 collective-permute-start.8
  61.2 7.9 %collective-permute-start.9 = (f32[2,16,128]{2,1,0:T(8,128)S(1)}, f32[2,16,128]{2,1,0:T(8,128)S(1)}, u32[]{:S(2)}, u32[]{:S(2)}) collective-permute-start(f32[2,16,128]{2,1,0:T(8,128)S(1)} %get-tuple-element.48), channel_id=1, source_target_pairs={{1,0},{2,1},{3,2},{4,3},{5,4},{6,5},{7,6},{8,7},{9,8},{10,9},{11,1... | collective-permute-start | bytes 49160 | tf_op jit(solution)/shard_map/ppermute | solution.py:27
  69.1 1.4 collective-permute-done.9
  70.5 0.4 fusion.2
  71.8 1.9 collective-permute-start.10
  73.7 7.9 %collective-permute-start.11 = (f32[2,16,128]{2,1,0:T(8,128)S(1)}, f32[2,16,128]{2,1,0:T(8,128)S(1)}, u32[]{:S(2)}, u32[]{:S(2)}) collective-permute-start(f32[2,16,128]{2,1,0:T(8,128)S(1)} %get-tuple-element.46), channel_id=1, source_target_pairs={{1,0},{2,1},{3,2},{4,3},{5,4},{6,5},{7,6},{8,7},{9,8},{10,9},{11,1... | collective-permute-start | bytes 49160 | tf_op jit(solution)/shard_map/ppermute | solution.py:27
  81.6 1.4 collective-permute-done.11
  84.3 1.9 collective-permute-start.12
  86.2 7.9 %collective-permute-start.13 = (f32[2,16,128]{2,1,0:T(8,128)S(1)}, f32[2,16,128]{2,1,0:T(8,128)S(1)}, u32[]{:S(2)}, u32[]{:S(2)}) collective-permute-start(f32[2,16,128]{2,1,0:T(8,128)S(1)} %get-tuple-element.44), channel_id=1, source_target_pairs={{1,0},{2,1},{3,2},{4,3},{5,4},{6,5},{7,6},{8,7},{9,8},{10,9},{11,1... | collective-permute-start | bytes 49160 | tf_op jit(solution)/shard_map/ppermute | solution.py:27
  94.1 1.4 collective-permute-done.13
  95.5 0.4 fusion.4
  96.8 1.9 collective-permute-start.14
  98.7 7.9 %collective-permute-start.15 = (f32[2,16,128]{2,1,0:T(8,128)S(1)}, f32[2,16,128]{2,1,0:T(8,128)S(1)}, u32[]{:S(2)}, u32[]{:S(2)}) collective-permute-start(f32[2,16,128]{2,1,0:T(8,128)S(1)} %get-tuple-element.42), channel_id=1, source_target_pairs={{1,0},{2,1},{3,2},{4,3},{5,4},{6,5},{7,6},{8,7},{9,8},{10,9},{11,1... | collective-permute-start | bytes 49160 | tf_op jit(solution)/shard_map/ppermute | solution.py:27
  106.6 1.4 collective-permute-done.15
  109.2 1.9 collective-permute-start.16
  111.2 7.9 %collective-permute-start.17 = (f32[2,16,128]{2,1,0:T(8,128)S(1)}, f32[2,16,128]{2,1,0:T(8,128)S(1)}, u32[]{:S(2)}, u32[]{:S(2)}) collective-permute-start(f32[2,16,128]{2,1,0:T(8,128)S(1)} %get-tuple-element.40), channel_id=1, source_target_pairs={{1,0},{2,1},{3,2},{4,3},{5,4},{6,5},{7,6},{8,7},{9,8},{10,9},{11,1... | collective-permute-start | bytes 49160 | tf_op jit(solution)/shard_map/ppermute | solution.py:27
  119.0 1.4 collective-permute-done.17
  120.5 0.4 fusion.6
  121.7 1.9 collective-permute-start.18
  123.7 7.9 %collective-permute-start.19 = (f32[2,16,128]{2,1,0:T(8,128)S(1)}, f32[2,16,128]{2,1,0:T(8,128)S(1)}, u32[]{:S(2)}, u32[]{:S(2)}) collective-permute-start(f32[2,16,128]{2,1,0:T(8,128)S(1)} %get-tuple-element.38), channel_id=1, source_target_pairs={{1,0},{2,1},{3,2},{4,3},{5,4},{6,5},{7,6},{8,7},{9,8},{10,9},{11,1... | collective-permute-start | bytes 49160 | tf_op jit(solution)/shard_map/ppermute | solution.py:27
  131.5 1.4 collective-permute-done.19
  134.2 1.9 collective-permute-start.20
  136.1 7.9 %collective-permute-start.21 = (f32[2,16,128]{2,1,0:T(8,128)S(1)}, f32[2,16,128]{2,1,0:T(8,128)S(1)}, u32[]{:S(2)}, u32[]{:S(2)}) collective-permute-start(f32[2,16,128]{2,1,0:T(8,128)S(1)} %get-tuple-element.36), channel_id=1, source_target_pairs={{1,0},{2,1},{3,2},{4,3},{5,4},{6,5},{7,6},{8,7},{9,8},{10,9},{11,1... | collective-permute-start | bytes 49160 | tf_op jit(solution)/shard_map/ppermute | solution.py:27
  144.0 1.4 collective-permute-done.21
  145.4 0.4 fusion.8
  146.7 1.9 collective-permute-start.22
  148.6 7.9 %collective-permute-start.23 = (f32[2,16,128]{2,1,0:T(8,128)S(1)}, f32[2,16,128]{2,1,0:T(8,128)S(1)}, u32[]{:S(2)}, u32[]{:S(2)}) collective-permute-start(f32[2,16,128]{2,1,0:T(8,128)S(1)} %get-tuple-element.34), channel_id=1, source_target_pairs={{1,0},{2,1},{3,2},{4,3},{5,4},{6,5},{7,6},{8,7},{9,8},{10,9},{11,1... | collective-permute-start | bytes 49160 | tf_op jit(solution)/shard_map/ppermute | solution.py:27
  156.5 1.4 collective-permute-done.23
  159.2 1.9 collective-permute-start.24
  161.1 7.9 %collective-permute-start.25 = (f32[2,16,128]{2,1,0:T(8,128)S(1)}, f32[2,16,128]{2,1,0:T(8,128)S(1)}, u32[]{:S(2)}, u32[]{:S(2)}) collective-permute-start(f32[2,16,128]{2,1,0:T(8,128)S(1)} %get-tuple-element.32), channel_id=1, source_target_pairs={{1,0},{2,1},{3,2},{4,3},{5,4},{6,5},{7,6},{8,7},{9,8},{10,9},{11,1... | collective-permute-start | bytes 49160 | tf_op jit(solution)/shard_map/ppermute | solution.py:27
  169.0 1.4 collective-permute-done.25
  170.4 0.4 fusion.10
  171.7 1.9 collective-permute-start.26
  173.6 7.9 %collective-permute-start.27 = (f32[2,16,128]{2,1,0:T(8,128)S(1)}, f32[2,16,128]{2,1,0:T(8,128)S(1)}, u32[]{:S(2)}, u32[]{:S(2)}) collective-permute-start(f32[2,16,128]{2,1,0:T(8,128)S(1)} %get-tuple-element.30), channel_id=1, source_target_pairs={{1,0},{2,1},{3,2},{4,3},{5,4},{6,5},{7,6},{8,7},{9,8},{10,9},{11,1... | collective-permute-start | bytes 49160 | tf_op jit(solution)/shard_map/ppermute | solution.py:27
  181.5 1.4 collective-permute-done.27
  182.9 0.4 fusion.11
  184.2 1.9 collective-permute-start.28
  186.1 7.9 %collective-permute-start.29 = (f32[2,16,128]{2,1,0:T(8,128)S(1)}, f32[2,16,128]{2,1,0:T(8,128)S(1)}, u32[]{:S(2)}, u32[]{:S(2)}) collective-permute-start(f32[2,16,128]{2,1,0:T(8,128)S(1)} %get-tuple-element.28), channel_id=1, source_target_pairs={{1,0},{2,1},{3,2},{4,3},{5,4},{6,5},{7,6},{8,7},{9,8},{10,9},{11,1... | collective-permute-start | bytes 49160 | tf_op jit(solution)/shard_map/ppermute | solution.py:27
  194.0 19.4 %all-reduce.27 = (f32[32]{0:T(128)S(1)}, f32[32]{0:T(128)S(1)}) all-reduce(f32[32]{0:T(128)S(1)} %get-tuple-element.11, f32[32]{0:T(128)S(1)} %get-tuple-element.10), channel_id=1, replica_groups=mesh['frames'=8,'slab'=32] {'frames'}, use_global_device_ids=true, to_apply=%region_28.29 | all-reduce | flops 64 | bytes 512 | tf_op jit(solution)/shard_map/psum | solution.py:125
  213.4 0.6 subtract_divide_fusion
  214.0 0.6 slice_subtract_fusion
  (151 shorter events, 13.4 us)
Async XLA Ops:
  1.3 22.3 %collective-permute-start = (bf16[2,4,128]{2,1,0:T(4,128)(2,1)S(1)}, bf16[2,4,128]{2,1,0:T(4,128)(2,1)S(1)}, u32[]{:S(2)}, u32[]{:S(2)}) collective-permute-start(bf16[2,4,128]{2,1,0:T(4,128)(2,1)S(1)} %get-tuple-element.55), channel_id=1, source_target_pairs={{0,1},{1,2},{2,3},{3,4},{4,5},{5,6},{6,7},{7,8},{8,9},{9,10},{10,1... | collective-permute-start | bytes 6152 | tf_op jit(solution)/shard_map/ppermute | solution.py:24
  3.3 20.4 %collective-permute-start.1 = (bf16[2,4,128]{2,1,0:T(4,128)(2,1)S(1)}, bf16[2,4,128]{2,1,0:T(4,128)(2,1)S(1)}, u32[]{:S(2)}, u32[]{:S(2)}) collective-permute-start(bf16[2,4,128]{2,1,0:T(4,128)(2,1)S(1)} %get-tuple-element.56), channel_id=1, source_target_pairs={{1,0},{2,1},{3,2},{4,3},{5,4},{6,5},{7,6},{8,7},{9,8},{10,9},{11,1... | collective-permute-start | bytes 6152 | tf_op jit(solution)/shard_map/ppermute | solution.py:27
  11.1 0.7 copy-start.4
  11.8 0.7 copy-start.2
  11.8 0.8 copy-start
  13.6 9.9 %copy-start.5 = (s32[32]{0:T(128)S(1)}, s32[32]{0:T(128)}, u32[]{:S(2)}) copy-start(s32[32]{0:T(128)} %param.10) | copy-start | bytes 388
  13.6 9.9 %copy-start.3 = (s32[2,2,2,1]{2,3,1,0:T(1,128)S(1)}, s32[2,2,2,1]{2,3,1,0:T(1,128)}, u32[]{:S(2)}) copy-start(s32[2,2,2,1]{2,3,1,0:T(1,128)} %param.7) | copy-start | bytes 100
  13.6 10.0 %copy-start.1 = (bf16[2,64,128]{2,1,0:T(8,128)(2,1)S(1)}, bf16[2,64,128]{2,1,0:T(8,128)(2,1)}, u32[]{:S(2)}) copy-start(bf16[2,64,128]{2,1,0:T(8,128)(2,1)} %param.6) | copy-start | bytes 98308
  13.6 32.0 %collective-permute-start.4 = (f32[2,16,128]{2,1,0:T(8,128)S(1)}, f32[2,16,128]{2,1,0:T(8,128)S(1)}, u32[]{:S(2)}, u32[]{:S(2)}) collective-permute-start(f32[2,16,128]{2,1,0:T(8,128)S(1)} %get-tuple-element.51), channel_id=1, source_target_pairs={{0,1},{1,2},{2,3},{3,4},{4,5},{5,6},{6,7},{7,8},{8,9},{9,10},{10,1... | collective-permute-start | bytes 49160 | tf_op jit(solution)/shard_map/ppermute | solution.py:24
  15.5 30.0 %collective-permute-start.5 = (f32[2,16,128]{2,1,0:T(8,128)S(1)}, f32[2,16,128]{2,1,0:T(8,128)S(1)}, u32[]{:S(2)}, u32[]{:S(2)}) collective-permute-start(f32[2,16,128]{2,1,0:T(8,128)S(1)} %get-tuple-element.52), channel_id=1, source_target_pairs={{1,0},{2,1},{3,2},{4,3},{5,4},{6,5},{7,6},{8,7},{9,8},{10,9},{11,1... | collective-permute-start | bytes 49160 | tf_op jit(solution)/shard_map/ppermute | solution.py:27
  34.5 9.9 %collective-permute-start.2 = (bf16[2,8,128]{2,1,0:T(8,128)(2,1)S(1)}, bf16[2,8,128]{2,1,0:T(8,128)(2,1)S(1)}, u32[]{:S(2)}, u32[]{:S(2)}) collective-permute-start(bf16[2,8,128]{2,1,0:T(8,128)(2,1)S(1)} %get-tuple-element.53), channel_id=1, source_target_pairs={{0,1},{1,2},{2,3},{3,4},{4,5},{5,6},{6,7},{7,8},{8,9},{9,10},{10,1... | collective-permute-start | bytes 12296 | tf_op jit(solution)/shard_map/ppermute | solution.py:24
  36.4 9.2 %collective-permute-start.3 = (bf16[2,8,128]{2,1,0:T(8,128)(2,1)S(1)}, bf16[2,8,128]{2,1,0:T(8,128)(2,1)S(1)}, u32[]{:S(2)}, u32[]{:S(2)}) collective-permute-start(bf16[2,8,128]{2,1,0:T(8,128)(2,1)S(1)} %get-tuple-element.54), channel_id=1, source_target_pairs={{1,0},{2,1},{3,2},{4,3},{5,4},{6,5},{7,6},{8,7},{9,8},{10,9},{11,1... | collective-permute-start | bytes 12296 | tf_op jit(solution)/shard_map/ppermute | solution.py:27
  46.8 9.8 %collective-permute-start.6 = (f32[2,16,128]{2,1,0:T(8,128)S(1)}, f32[2,16,128]{2,1,0:T(8,128)S(1)}, u32[]{:S(2)}, u32[]{:S(2)}) collective-permute-start(f32[2,16,128]{2,1,0:T(8,128)S(1)} %get-tuple-element.49), channel_id=1, source_target_pairs={{0,1},{1,2},{2,3},{3,4},{4,5},{5,6},{6,7},{7,8},{8,9},{9,10},{10,1... | collective-permute-start | bytes 49160 | tf_op jit(solution)/shard_map/ppermute | solution.py:24
  48.8 9.3 %collective-permute-start.7 = (f32[2,16,128]{2,1,0:T(8,128)S(1)}, f32[2,16,128]{2,1,0:T(8,128)S(1)}, u32[]{:S(2)}, u32[]{:S(2)}) collective-permute-start(f32[2,16,128]{2,1,0:T(8,128)S(1)} %get-tuple-element.50), channel_id=1, source_target_pairs={{1,0},{2,1},{3,2},{4,3},{5,4},{6,5},{7,6},{8,7},{9,8},{10,9},{11,1... | collective-permute-start | bytes 49160 | tf_op jit(solution)/shard_map/ppermute | solution.py:27
  59.3 9.8 %collective-permute-start.8 = (f32[2,16,128]{2,1,0:T(8,128)S(1)}, f32[2,16,128]{2,1,0:T(8,128)S(1)}, u32[]{:S(2)}, u32[]{:S(2)}) collective-permute-start(f32[2,16,128]{2,1,0:T(8,128)S(1)} %get-tuple-element.47), channel_id=1, source_target_pairs={{0,1},{1,2},{2,3},{3,4},{4,5},{5,6},{6,7},{7,8},{8,9},{9,10},{10,1... | collective-permute-start | bytes 49160 | tf_op jit(solution)/shard_map/ppermute | solution.py:24
  61.2 9.3 %collective-permute-start.9 = (f32[2,16,128]{2,1,0:T(8,128)S(1)}, f32[2,16,128]{2,1,0:T(8,128)S(1)}, u32[]{:S(2)}, u32[]{:S(2)}) collective-permute-start(f32[2,16,128]{2,1,0:T(8,128)S(1)} %get-tuple-element.48), channel_id=1, source_target_pairs={{1,0},{2,1},{3,2},{4,3},{5,4},{6,5},{7,6},{8,7},{9,8},{10,9},{11,1... | collective-permute-start | bytes 49160 | tf_op jit(solution)/shard_map/ppermute | solution.py:27
  71.8 9.8 %collective-permute-start.10 = (f32[2,16,128]{2,1,0:T(8,128)S(1)}, f32[2,16,128]{2,1,0:T(8,128)S(1)}, u32[]{:S(2)}, u32[]{:S(2)}) collective-permute-start(f32[2,16,128]{2,1,0:T(8,128)S(1)} %get-tuple-element.45), channel_id=1, source_target_pairs={{0,1},{1,2},{2,3},{3,4},{4,5},{5,6},{6,7},{7,8},{8,9},{9,10},{10,1... | collective-permute-start | bytes 49160 | tf_op jit(solution)/shard_map/ppermute | solution.py:24
  73.7 9.3 %collective-permute-start.11 = (f32[2,16,128]{2,1,0:T(8,128)S(1)}, f32[2,16,128]{2,1,0:T(8,128)S(1)}, u32[]{:S(2)}, u32[]{:S(2)}) collective-permute-start(f32[2,16,128]{2,1,0:T(8,128)S(1)} %get-tuple-element.46), channel_id=1, source_target_pairs={{1,0},{2,1},{3,2},{4,3},{5,4},{6,5},{7,6},{8,7},{9,8},{10,9},{11,1... | collective-permute-start | bytes 49160 | tf_op jit(solution)/shard_map/ppermute | solution.py:27
  84.3 9.8 %collective-permute-start.12 = (f32[2,16,128]{2,1,0:T(8,128)S(1)}, f32[2,16,128]{2,1,0:T(8,128)S(1)}, u32[]{:S(2)}, u32[]{:S(2)}) collective-permute-start(f32[2,16,128]{2,1,0:T(8,128)S(1)} %get-tuple-element.43), channel_id=1, source_target_pairs={{0,1},{1,2},{2,3},{3,4},{4,5},{5,6},{6,7},{7,8},{8,9},{9,10},{10,1... | collective-permute-start | bytes 49160 | tf_op jit(solution)/shard_map/ppermute | solution.py:24
  86.2 9.3 %collective-permute-start.13 = (f32[2,16,128]{2,1,0:T(8,128)S(1)}, f32[2,16,128]{2,1,0:T(8,128)S(1)}, u32[]{:S(2)}, u32[]{:S(2)}) collective-permute-start(f32[2,16,128]{2,1,0:T(8,128)S(1)} %get-tuple-element.44), channel_id=1, source_target_pairs={{1,0},{2,1},{3,2},{4,3},{5,4},{6,5},{7,6},{8,7},{9,8},{10,9},{11,1... | collective-permute-start | bytes 49160 | tf_op jit(solution)/shard_map/ppermute | solution.py:27
  96.8 9.8 %collective-permute-start.14 = (f32[2,16,128]{2,1,0:T(8,128)S(1)}, f32[2,16,128]{2,1,0:T(8,128)S(1)}, u32[]{:S(2)}, u32[]{:S(2)}) collective-permute-start(f32[2,16,128]{2,1,0:T(8,128)S(1)} %get-tuple-element.41), channel_id=1, source_target_pairs={{0,1},{1,2},{2,3},{3,4},{4,5},{5,6},{6,7},{7,8},{8,9},{9,10},{10,1... | collective-permute-start | bytes 49160 | tf_op jit(solution)/shard_map/ppermute | solution.py:24
  98.7 9.3 %collective-permute-start.15 = (f32[2,16,128]{2,1,0:T(8,128)S(1)}, f32[2,16,128]{2,1,0:T(8,128)S(1)}, u32[]{:S(2)}, u32[]{:S(2)}) collective-permute-start(f32[2,16,128]{2,1,0:T(8,128)S(1)} %get-tuple-element.42), channel_id=1, source_target_pairs={{1,0},{2,1},{3,2},{4,3},{5,4},{6,5},{7,6},{8,7},{9,8},{10,9},{11,1... | collective-permute-start | bytes 49160 | tf_op jit(solution)/shard_map/ppermute | solution.py:27
  109.2 9.8 %collective-permute-start.16 = (f32[2,16,128]{2,1,0:T(8,128)S(1)}, f32[2,16,128]{2,1,0:T(8,128)S(1)}, u32[]{:S(2)}, u32[]{:S(2)}) collective-permute-start(f32[2,16,128]{2,1,0:T(8,128)S(1)} %get-tuple-element.39), channel_id=1, source_target_pairs={{0,1},{1,2},{2,3},{3,4},{4,5},{5,6},{6,7},{7,8},{8,9},{9,10},{10,1... | collective-permute-start | bytes 49160 | tf_op jit(solution)/shard_map/ppermute | solution.py:24
  111.2 9.3 %collective-permute-start.17 = (f32[2,16,128]{2,1,0:T(8,128)S(1)}, f32[2,16,128]{2,1,0:T(8,128)S(1)}, u32[]{:S(2)}, u32[]{:S(2)}) collective-permute-start(f32[2,16,128]{2,1,0:T(8,128)S(1)} %get-tuple-element.40), channel_id=1, source_target_pairs={{1,0},{2,1},{3,2},{4,3},{5,4},{6,5},{7,6},{8,7},{9,8},{10,9},{11,1... | collective-permute-start | bytes 49160 | tf_op jit(solution)/shard_map/ppermute | solution.py:27
  121.7 9.8 %collective-permute-start.18 = (f32[2,16,128]{2,1,0:T(8,128)S(1)}, f32[2,16,128]{2,1,0:T(8,128)S(1)}, u32[]{:S(2)}, u32[]{:S(2)}) collective-permute-start(f32[2,16,128]{2,1,0:T(8,128)S(1)} %get-tuple-element.37), channel_id=1, source_target_pairs={{0,1},{1,2},{2,3},{3,4},{4,5},{5,6},{6,7},{7,8},{8,9},{9,10},{10,1... | collective-permute-start | bytes 49160 | tf_op jit(solution)/shard_map/ppermute | solution.py:24
  123.7 9.3 %collective-permute-start.19 = (f32[2,16,128]{2,1,0:T(8,128)S(1)}, f32[2,16,128]{2,1,0:T(8,128)S(1)}, u32[]{:S(2)}, u32[]{:S(2)}) collective-permute-start(f32[2,16,128]{2,1,0:T(8,128)S(1)} %get-tuple-element.38), channel_id=1, source_target_pairs={{1,0},{2,1},{3,2},{4,3},{5,4},{6,5},{7,6},{8,7},{9,8},{10,9},{11,1... | collective-permute-start | bytes 49160 | tf_op jit(solution)/shard_map/ppermute | solution.py:27
  134.2 9.8 %collective-permute-start.20 = (f32[2,16,128]{2,1,0:T(8,128)S(1)}, f32[2,16,128]{2,1,0:T(8,128)S(1)}, u32[]{:S(2)}, u32[]{:S(2)}) collective-permute-start(f32[2,16,128]{2,1,0:T(8,128)S(1)} %get-tuple-element.35), channel_id=1, source_target_pairs={{0,1},{1,2},{2,3},{3,4},{4,5},{5,6},{6,7},{7,8},{8,9},{9,10},{10,1... | collective-permute-start | bytes 49160 | tf_op jit(solution)/shard_map/ppermute | solution.py:24
  136.1 9.3 %collective-permute-start.21 = (f32[2,16,128]{2,1,0:T(8,128)S(1)}, f32[2,16,128]{2,1,0:T(8,128)S(1)}, u32[]{:S(2)}, u32[]{:S(2)}) collective-permute-start(f32[2,16,128]{2,1,0:T(8,128)S(1)} %get-tuple-element.36), channel_id=1, source_target_pairs={{1,0},{2,1},{3,2},{4,3},{5,4},{6,5},{7,6},{8,7},{9,8},{10,9},{11,1... | collective-permute-start | bytes 49160 | tf_op jit(solution)/shard_map/ppermute | solution.py:27
  146.7 9.8 %collective-permute-start.22 = (f32[2,16,128]{2,1,0:T(8,128)S(1)}, f32[2,16,128]{2,1,0:T(8,128)S(1)}, u32[]{:S(2)}, u32[]{:S(2)}) collective-permute-start(f32[2,16,128]{2,1,0:T(8,128)S(1)} %get-tuple-element.33), channel_id=1, source_target_pairs={{0,1},{1,2},{2,3},{3,4},{4,5},{5,6},{6,7},{7,8},{8,9},{9,10},{10,1... | collective-permute-start | bytes 49160 | tf_op jit(solution)/shard_map/ppermute | solution.py:24
  148.6 9.3 %collective-permute-start.23 = (f32[2,16,128]{2,1,0:T(8,128)S(1)}, f32[2,16,128]{2,1,0:T(8,128)S(1)}, u32[]{:S(2)}, u32[]{:S(2)}) collective-permute-start(f32[2,16,128]{2,1,0:T(8,128)S(1)} %get-tuple-element.34), channel_id=1, source_target_pairs={{1,0},{2,1},{3,2},{4,3},{5,4},{6,5},{7,6},{8,7},{9,8},{10,9},{11,1... | collective-permute-start | bytes 49160 | tf_op jit(solution)/shard_map/ppermute | solution.py:27
  159.2 9.8 %collective-permute-start.24 = (f32[2,16,128]{2,1,0:T(8,128)S(1)}, f32[2,16,128]{2,1,0:T(8,128)S(1)}, u32[]{:S(2)}, u32[]{:S(2)}) collective-permute-start(f32[2,16,128]{2,1,0:T(8,128)S(1)} %get-tuple-element.31), channel_id=1, source_target_pairs={{0,1},{1,2},{2,3},{3,4},{4,5},{5,6},{6,7},{7,8},{8,9},{9,10},{10,1... | collective-permute-start | bytes 49160 | tf_op jit(solution)/shard_map/ppermute | solution.py:24
  161.1 9.3 %collective-permute-start.25 = (f32[2,16,128]{2,1,0:T(8,128)S(1)}, f32[2,16,128]{2,1,0:T(8,128)S(1)}, u32[]{:S(2)}, u32[]{:S(2)}) collective-permute-start(f32[2,16,128]{2,1,0:T(8,128)S(1)} %get-tuple-element.32), channel_id=1, source_target_pairs={{1,0},{2,1},{3,2},{4,3},{5,4},{6,5},{7,6},{8,7},{9,8},{10,9},{11,1... | collective-permute-start | bytes 49160 | tf_op jit(solution)/shard_map/ppermute | solution.py:27
  171.7 9.8 %collective-permute-start.26 = (f32[2,16,128]{2,1,0:T(8,128)S(1)}, f32[2,16,128]{2,1,0:T(8,128)S(1)}, u32[]{:S(2)}, u32[]{:S(2)}) collective-permute-start(f32[2,16,128]{2,1,0:T(8,128)S(1)} %get-tuple-element.29), channel_id=1, source_target_pairs={{0,1},{1,2},{2,3},{3,4},{4,5},{5,6},{6,7},{7,8},{8,9},{9,10},{10,1... | collective-permute-start | bytes 49160 | tf_op jit(solution)/shard_map/ppermute | solution.py:24
  173.6 9.3 %collective-permute-start.27 = (f32[2,16,128]{2,1,0:T(8,128)S(1)}, f32[2,16,128]{2,1,0:T(8,128)S(1)}, u32[]{:S(2)}, u32[]{:S(2)}) collective-permute-start(f32[2,16,128]{2,1,0:T(8,128)S(1)} %get-tuple-element.30), channel_id=1, source_target_pairs={{1,0},{2,1},{3,2},{4,3},{5,4},{6,5},{7,6},{8,7},{9,8},{10,9},{11,1... | collective-permute-start | bytes 49160 | tf_op jit(solution)/shard_map/ppermute | solution.py:27
  184.2 29.8 %collective-permute-start.28 = (f32[2,16,128]{2,1,0:T(8,128)S(1)}, f32[2,16,128]{2,1,0:T(8,128)S(1)}, u32[]{:S(2)}, u32[]{:S(2)}) collective-permute-start(f32[2,16,128]{2,1,0:T(8,128)S(1)} %get-tuple-element.27), channel_id=1, source_target_pairs={{0,1},{1,2},{2,3},{3,4},{4,5},{5,6},{6,7},{7,8},{8,9},{9,10},{10,1... | collective-permute-start | bytes 49160 | tf_op jit(solution)/shard_map/ppermute | solution.py:24
  186.1 27.9 %collective-permute-start.29 = (f32[2,16,128]{2,1,0:T(8,128)S(1)}, f32[2,16,128]{2,1,0:T(8,128)S(1)}, u32[]{:S(2)}, u32[]{:S(2)}) collective-permute-start(f32[2,16,128]{2,1,0:T(8,128)S(1)} %get-tuple-element.28), channel_id=1, source_target_pairs={{1,0},{2,1},{3,2},{4,3},{5,4},{6,5},{7,6},{8,7},{9,8},{10,9},{11,1... | collective-permute-start | bytes 49160 | tf_op jit(solution)/shard_map/ppermute | solution.py:27
where the time goes:
time: 216 us; the launch traced here: 215 us
  starting transfers between devices  147 us (68%)
  blocking collectives  19.4 us (9%)
  waiting for transfers between devices  16.8 us (8%)
  local copies, waits for them, and re-layouts  16.2 us (8%)
  matrix products  11.1 us (5%)
  other arithmetic  2.88 us (1%)
    ppermute x15, starting transfers between devices, extended(): lax.ppermute(lax.slice_in_dim(block, 0, width, axis=dim), axis, backward)  118 us
    ppermute x15, starting transfers between devices, extended(): lax.ppermute(lax.slice_in_dim(block, block.shape[dim] - width, None, axis...  28.8 us
    psum x1, blocking collectives, shards(): lax.psum((jnp.sum(traces, axis=1), jnp.sum(traces * traces, axis=1)), 'fr...  19.4 us
    ppermute x15, waiting for transfers between devices, extended(): lax.ppermute(lax.slice_in_dim(block, 0, width, axis=dim), axis, backward)  16.8 us
    gather x12, local copies, waits for them, and re-layouts  10.7 us
    dot_general x13, matrix products, render_with(): return jnp.einsum('tyr,rx->tyx', mixed, col_placed, precision=HIGHEST)  5.58 us
    dot_general x12, matrix products, project_with(): jnp.einsum('tyx,rx->tyr', residual, col_placed, precision=HIGHEST)  5.26 us
  transfers between devices with their start and end apart: 30, of which 12 were waited for; matrix products, arithmetic and copies ran while one was open for 6% of the time, Pallas kernels for 0%

commit v1 on v0

v1 whole, which is shorter than its diff:
```python
import functools

import jax
import jax.numpy as jnp
from jax import lax
from jax.experimental import pallas as pl
from jax.experimental.pallas import tpu as pltpu
from jax.sharding import PartitionSpec as P

ROWS = 64
COLS = 128
KD = 32
TILE = 16
RIM = 8
EXT = 80
BLOCKS = 4
SWEEPS = 3
STEPS = BLOCKS * SWEEPS
HALO = STEPS
SLOTS = 2 * HALO + 1
CHUNKS = (SLOTS + 3) // 4
EPSILON = 1e-05
MESH = pl.DeviceIdType.MESH
F32 = jnp.float32
BF16 = jnp.bfloat16
NT = (((1,), (1,)), ((), ()))


def iota(shape, dim):
    return lax.broadcasted_iota(jnp.int32, shape, dim)


def mm(a, b):
    return jnp.dot(a, b, preferred_element_type=F32)


def mm_nt(a, b):
    return lax.dot_general(a, b, NT, preferred_element_type=F32)


def split(x):
    hi = x.astype(BF16).astype(F32)
    return hi, x - hi


def place_columns(packed, col, wide_ref):
    lane_group = iota((TILE, COLS), 1) // TILE
    for g in range(4):
        rows = packed[g * TILE : (g + 1) * TILE, :]
        lhs = jnp.concatenate(
            [jnp.where(lane_group == kk, rows, 0.0).astype(BF16) for kk in range(8)], axis=0
        )
        anchor = jnp.broadcast_to(col[8 * g : 8 * g + 8, None, :], (8, TILE, COLS))
        offset = (iota((8, TILE, COLS), 2) - iota((8, TILE, COLS), 1)).astype(F32)
        onehot = jnp.where(anchor == offset, 1.0, 0.0).astype(BF16).reshape(COLS, COLS)
        wide_ref[g * COLS : (g + 1) * COLS, :] = mm(lhs, onehot)


def place_rows(row, wide_ref, first, count):
    known = {}
    bits = [((row >> b) & 1) == 1 for b in range(6)]

    def at(level, y):
        if y < 0 or y > TILE - 1 + (1 << level) - 1:
            return None
        if level == 0:
            if (0, y) not in known:
                known[0, y] = wide_ref[pl.ds(y, KD, stride=TILE), :]
            return known[0, y]
        if (level, y) not in known:
            moved = at(level - 1, y - (1 << (level - 1)))
            kept = at(level - 1, y)
            zero = jnp.zeros((KD, COLS), F32)
            bit = bits[level - 1]
            known[level, y] = jnp.where(
                bit, zero if moved is None else moved, zero if kept is None else kept
            )
        return known[level, y]

    return [at(6, y) for y in range(first, first + count)]


def kernel(
    n_slab,
    n_frames,
    raw_ref,
    shift_ref,
    foot_ref,
    anchor_ref,
    block_ref,
    trace_ref,
    z_ref,
    res_ref,
    pkt_out,
    pkt_in,
    inbox,
    mom_out,
    mom_in,
    wide,
    image,
    rawx,
    mixed,
    corr,
    band,
    xrow,
    e1_send,
    e1_recv,
    e2_send,
    e2_recv,
    e3_send,
    e3_recv,
):
    me = lax.axis_index("slab")
    frame = lax.axis_index("frames")

    def slab_at(offset):
        return lax.rem(me + offset + 2 * n_slab, n_slab)

    def frame_at(offset):
        return lax.rem(frame + offset, n_frames)

    barrier = pltpu.get_barrier_semaphore()

    def greet_slab(i, carry):
        for sign in (1, -1):
            pl.semaphore_signal(
                barrier, 1, device_id={"slab": slab_at(sign * i)}, device_id_type=MESH
            )
        return carry

    def greet_frame(i, carry):
        pl.semaphore_signal(barrier, 1, device_id={"frames": frame_at(i)}, device_id_type=MESH)
        return carry

    lax.fori_loop(1, HALO + 1, greet_slab, 0)
    lax.fori_loop(1, n_frames, greet_frame, 0)

    foot = foot_ref[...]
    packed = jnp.zeros((4 * TILE, COLS), F32)
    for kk in range(8):
        piece = jnp.concatenate([foot[8 * g + kk] for g in range(4)], axis=0)
        spread = jnp.where(iota((TILE, COLS), 1) - kk * TILE == iota((TILE, COLS), 0), 1.0, 0.0)
        packed = packed + mm(piece, spread.astype(BF16))
    packed = packed.astype(BF16)
    own_row = (anchor_ref[:, 0:1] - (me * ROWS - RIM)) + jnp.zeros((KD, COLS), jnp.int32)
    own_col = (anchor_ref[:, 1:2] + jnp.zeros((KD, COLS), jnp.int32)).astype(F32)
    start = trace_ref[...]
    t_hi, t_rest = split(start)
    t_mid, t_lo = split(t_rest)
    lane = iota((KD, COLS), 1)
    small = jnp.where(lane == 0, own_row.astype(F32), 0.0)
    small = jnp.where(lane == 1, own_col, small)
    for i, part in enumerate((t_hi, t_mid, t_lo)):
        for t in range(2):
            small = jnp.where(lane == 2 + 2 * i + t, part[:, t : t + 1], small)
    for side, patch in ((0, 0), (1, 1)):
        mine = small
        for which in range(2):
            for t in range(2):
                value = jnp.full((KD, COLS), shift_ref[which, t, patch, 0], jnp.int32).astype(F32)
                mine = jnp.where(lane == 8 + 2 * which + t, value, mine)
        top = 0 if side == 0 else ROWS - 16
        for t in range(2):
            pkt_out[side, 16 * t : 16 * t + 16, :] = raw_ref[t, top : top + 16, :]
        pkt_out[side, 32:96, :] = packed
        pkt_out[side, 96:128, :] = mine.astype(BF16)

    pl.semaphore_wait(barrier, 2 * HALO + n_frames - 1)

    def packet(side):
        return pltpu.make_async_remote_copy(
            src_ref=pkt_out.at[side],
            dst_ref=pkt_in.at[1 - side],
            send_sem=e1_send.at[side],
            recv_sem=e1_recv.at[1 - side],
            device_id={"slab": slab_at(-1 if side == 0 else 1)},
            device_id_type=MESH,
        )

    to_left, to_right = packet(0), packet(1)
    to_left.start()
    to_right.start()

    image[...] = jnp.zeros(image.shape, BF16)
    place_columns(packed, own_col, wide)
    for y, value in enumerate(place_rows(own_row, wide, 0, EXT)):
        if value is not None:
            image[0:KD, y * COLS : (y + 1) * COLS] = value.astype(BF16)
    own = image[0:KD, :]
    gram_own = mm_nt(own, own)
    eye = iota((KD, KD), 0) == iota((KD, KD), 1)
    norm_sq = jnp.sum(jnp.where(eye, gram_own, 0.0), axis=0, keepdims=True)
    for t in range(2):
        rawx[t * 96 + 16 : t * 96 + 80, :] = raw_ref[t].astype(F32)

    to_left.wait()
    to_right.wait()

    smalls = []
    valid = []
    for side in range(2):
        inside = me > 0 if side == 0 else me < n_slab - 1
        keep = jnp.where(inside, 1.0, 0.0).astype(F32)
        valid.append(keep)
        info = pkt_in[side, 96:128, :].astype(F32) * keep
        smalls.append(info)
        place_columns(
            pkt_in[side, 32:96, :], info[:, 1:2] + jnp.zeros((KD, COLS), F32), wide
        )
        row = (info[:, 0:1] + jnp.zeros((KD, COLS), F32)).astype(jnp.int32)
        first = ROWS if side == 0 else 0
        low = 96 if side == 0 else 32
        for i, value in enumerate(place_rows(row, wide, first, 16)):
            if value is not None:
                y = i if side == 0 else ROWS + i
                image[low : low + KD, y * COLS : (y + 1) * COLS] = (value * keep).astype(BF16)
        for t in range(2):
            at = t * 96 + (0 if side == 0 else 80)
            rawx[at : at + 16, :] = pkt_in[side, 16 * t : 16 * t + 16, :].astype(F32) * keep
    gram_left = mm_nt(image[96:128, 0 : 16 * COLS], image[0:KD, 0 : 16 * COLS])
    gram_right = mm_nt(image[32:64, ROWS * COLS :], image[0:KD, ROWS * COLS :])

    for t in range(2):
        mixed[t * 96 : t * 96 + 88, :] = (
            0.75 * rawx[t * 96 + 4 : t * 96 + 92, :] + 0.25 * rawx[t * 96 + 5 : t * 96 + 93, :]
        )
        for y0, n in ((-RIM, RIM), (0, 32), (32, 32), (ROWS, RIM)):
            if 0 <= y0 < ROWS:
                down = jnp.full((n, COLS), shift_ref[0, t, y0 // 32, 0], jnp.int32).astype(F32)
                across = jnp.full((n, COLS), shift_ref[1, t, y0 // 32, 0], jnp.int32).astype(F32)
            else:
                info = smalls[0 if y0 < 0 else 1]
                down = jnp.broadcast_to(info[0:1, 8 + t : 9 + t], (n, COLS))
                across = jnp.broadcast_to(info[0:1, 10 + t : 11 + t], (n, COLS))
            picked = jnp.zeros((n, COLS), F32)
            for a in range(-3, 4):
                at = t * 96 + y0 + 12 + a
                picked = jnp.where(down == a, mixed[at : at + n, :], picked)
            place = iota((n, COLS), 1)
            moved = jnp.zeros((n, COLS), F32)
            for c in range(-3, 4):
                turned = picked if c == 0 else pltpu.roll(picked, (-c) % COLS, 1)
                within = (place + c >= 0) & (place + c < COLS)
                moved = jnp.where((across == c) & within, turned, moved)
            moved = moved.astype(BF16).astype(F32)
            if y0 < 0:
                moved = moved * valid[0]
            if y0 >= ROWS:
                moved = moved * valid[1]
            at = t * EXT + y0 + RIM
            corr[at : at + n, :] = moved
    corr[2 * EXT :, :] = jnp.zeros((6 * EXT, COLS), F32)
    frames_rows = jnp.concatenate([corr[pl.ds(y, 8, stride=EXT), :] for y in range(EXT)], axis=1)
    q = mm_nt(frames_rows.astype(BF16), image[0:KD, :])

    old = [start]
    for info in smalls:
        old.append(info[:, 2:4] + info[:, 4:6] + info[:, 6:8])
    grams = (gram_own, gram_left, gram_right)
    mine = inbox.at[HALO]
    mine[:, 0:32] = gram_left
    mine[:, 32:64] = gram_own
    mine[:, 64:96] = gram_right
    mine[:, 96:128] = jnp.zeros((KD, KD), F32)
    for t in range(2):
        rendered = sum(
            jnp.sum(gram * x[:, t : t + 1], axis=0, keepdims=True) for gram, x in zip(grams, old)
        )
        mine[t : t + 1, 96:128] = q[t : t + 1, :] - rendered
    mine[2:3, 96:128] = 1.0 / norm_sq
    mine[3:4, 96:128] = block_ref[...].astype(F32)

    def message(offset):
        slot = HALO - offset
        return pltpu.make_async_remote_copy(
            src_ref=inbox.at[HALO],
            dst_ref=inbox.at[slot],
            send_sem=e2_send.at[slot],
            recv_sem=e2_recv.at[slot],
            device_id={"slab": slab_at(offset)},
            device_id_type=MESH,
        )

    def send(i, carry):
        message(i).start()
        message(-i).start()
        return carry

    def arrive(i, carry):
        message(i).wait()
        message(-i).wait()
        return carry

    lax.fori_loop(1, HALO + 1, send, 0)

    lanes8 = iota((8, COLS), 1)
    wide_lane = iota((KD, COLS), 1)
    wide_row = iota((KD, COLS), 0)
    first_rows = []
    for x, low in zip(old, (0, 96, 32)):
        first_rows.append(
            [
                jnp.sum(
                    jnp.where(wide_lane - low == wide_row, x[:, t : t + 1], 0.0),
                    axis=0,
                    keepdims=True,
                )
                for t in range(2)
            ]
        )

    def rows_of(pair):
        sub = iota((8, COLS), 0)
        return jnp.where(sub == 0, pair[0], 0.0) + jnp.where(sub == 1, pair[1], 0.0)

    own_x, left_x, right_x = (rows_of(pair) for pair in first_rows)

    lax.fori_loop(1, HALO + 1, arrive, 0)

    def block_of_slot(slot, which, lane_chunk):
        value = inbox[slot]
        turn = (32 * (lane_chunk - which)) % COLS
        return value if turn == 0 else pltpu.roll(value, turn, 1)

    lane_chunk = wide_lane // 32
    scal = []
    for m in range(CHUNKS):
        keeps = []
        for i in range(4):
            slot = 4 * m + i
            if slot >= SLOTS:
                keeps.append(None)
                continue
            where = me + (slot - HALO)
            keeps.append(jnp.where((where >= 0) & (where < n_slab), 1.0, 0.0).astype(F32))
        tops = jnp.zeros((8, COLS), F32)
        for i in range(4):
            if keeps[i] is None:
                continue
            top = inbox[4 * m + i, 0:8, :]
            turn = (32 * (i - 3)) % COLS
            top = top if turn == 0 else pltpu.roll(top, turn, 1)
            tops = tops + jnp.where(lanes8 // 32 == i, top * keeps[i], 0.0)
        scal.append(tops)
        parts = []
        for rows in range(8):
            terms = []
            if rows < 4:
                terms = [(rows, 1), (rows + 1, 0), (rows - 1, 2)]
            elif rows == 4:
                terms = [(3, 2)]
            elif rows == 7:
                terms = [(0, 0)]
            total = jnp.zeros((KD, COLS), F32)
            for i, which in terms:
                if 0 <= i < 4 and keeps[i] is not None:
                    value = block_of_slot(4 * m + i, which, i) * keeps[i]
                    total = total + jnp.where(lane_chunk == i, value, 0.0)
            parts.append(total)
        for rows, total in enumerate(parts):
            hi, lo = split(total)
            band[m, rows * KD : (rows + 1) * KD, 0:COLS] = hi.astype(BF16)
            band[m, rows * KD : (rows + 1) * KD, COLS:] = lo.astype(BF16)

    state = list(scal)
    gains = [
        [
            jnp.where(tops[3:4, :] == float(b), tops[2:3, :], 0.0)
            for b in range(BLOCKS)
        ]
        for tops in scal
    ]
    total2 = jnp.where(lanes8 >= 96, left_x, 0.0)
    total3 = own_x + right_x
    for step in range(1, STEPS + 1):
        b = (step - 1) % BLOCKS
        low, high = max(step - 1, 0) // 4, min(2 * HALO + 1 - step, SLOTS - 1) // 4
        change = {m: state[m] * gains[m][b] for m in range(low, high + 1)}
        total2 = total2 + change[2]
        total3 = total3 + change[3]
        if step == STEPS:
            break
        zero = jnp.zeros((8, COLS), F32)
        for m in range(step // 4, (2 * HALO - step) // 4 + 1):
            beside = jnp.where(
                lanes8 >= 96,
                change.get(m - 1, zero),
                jnp.where(lanes8 < 32, change.get(m + 1, zero), 0.0),
            )
            a_hi, a_lo = split(change[m])
            b_hi, b_lo = split(beside)
            lhs = jnp.concatenate(
                [jnp.concatenate([a_hi, a_lo], axis=0), jnp.concatenate([b_hi, b_lo], axis=0)],
                axis=1,
            ).astype(BF16)
            out = mm(lhs, band[m])
            state[m] = state[m] - (out[0:8, 0:COLS] + out[8:16, 0:COLS] + out[0:8, COLS:])

    own_lane = lanes8 < 32
    two_rows = iota((8, COLS), 0) < 2
    final = jnp.where(own_lane & two_rows, total3, 0.0)
    mom_out[0:1, :] = jnp.sum(final, axis=0, keepdims=True)
    mom_out[1:2, :] = jnp.sum(final * final, axis=0, keepdims=True)
    mom_out[2:8, :] = jnp.zeros((6, COLS), F32)

    def moments(i):
        return pltpu.make_async_remote_copy(
            src_ref=mom_out,
            dst_ref=mom_in.at[n_frames - i],
            send_sem=e3_send.at[n_frames - i],
            recv_sem=e3_recv.at[n_frames - i],
            device_id={"frames": frame_at(i)},
            device_id_type=MESH,
        )

    def send_moments(i, carry):
        moments(i).start()
        return carry

    def arrive_moments(i, carry):
        moments(i).wait()
        return carry

    lax.fori_loop(1, n_frames, send_moments, 0)

    all_x = jnp.where(lanes8 < 64, total3, jnp.where(lanes8 >= 96, total2, 0.0))
    x_hi, x_lo = split(all_x)
    lhs = jnp.concatenate([x_hi, x_lo], axis=0).astype(BF16)
    pieces = (
        mm(lhs, image[:, RIM * COLS : 16 * COLS]),
        mm(lhs[:, 0:KD], image[0:KD, 16 * COLS : ROWS * COLS]),
        mm(lhs, image[:, ROWS * COLS : (ROWS + RIM) * COLS]),
    )
    y = 0
    for piece in pieces:
        rendered = piece[0:8, :] + piece[8:16, :]
        for i in range(piece.shape[1] // COLS):
            rows = corr[pl.ds(y + RIM, 8, stride=EXT), :] - rendered[:, i * COLS : (i + 1) * COLS]
            res_ref[pl.ds(y, 2, stride=ROWS), :] = rows[0:2, :]
            y += 1

    lax.fori_loop(1, n_frames, arrive_moments, 0)
    sums = mom_out[...]
    for i in range(1, n_frames):
        sums = sums + mom_in[i]
    count = 2 * n_frames
    mean = sums[0:1, :] / count
    square = sums[1:2, :] / count
    spread = square - mean * mean
    z_row = (total3[0:2, :] - mean) / jnp.sqrt(spread + EPSILON)
    pick = (wide_lane == wide_row) & (wide_lane < KD)
    cols = [
        jnp.sum(jnp.where(pick, z_row[t : t + 1, :], 0.0), axis=1, keepdims=True)
        for t in range(2)
    ]
    z_ref[:, 0:1] = cols[0]
    z_ref[:, 1:2] = cols[1]


def shards(n_slab, n_frames, raw_movie, shifts, footprints, anchors, block_of, init_traces):
    vmem = pl.BlockSpec(memory_space=pltpu.VMEM)
    smem = pl.BlockSpec(memory_space=pltpu.SMEM)
    dma = pltpu.SemaphoreType.DMA
    traces_z, residual = pl.pallas_call(
        functools.partial(kernel, n_slab, n_frames),
        out_shape=(
            jax.ShapeDtypeStruct((KD, 2), F32),
            jax.ShapeDtypeStruct((2 * ROWS, COLS), F32),
        ),
        in_specs=[vmem, smem, vmem, vmem, vmem, vmem],
        out_specs=(vmem, vmem),
        scratch_shapes=[
            pltpu.VMEM((2, 128, COLS), BF16),
            pltpu.VMEM((2, 128, COLS), BF16),
            pltpu.VMEM((SLOTS, KD, COLS), F32),
            pltpu.VMEM((8, COLS), F32),
            pltpu.VMEM((n_frames, 8, COLS), F32),
            pltpu.VMEM((KD * TILE, COLS), F32),
            pltpu.VMEM((128, EXT * COLS), BF16),
            pltpu.VMEM((192, COLS), F32),
            pltpu.VMEM((192, COLS), F32),
            pltpu.VMEM((8 * EXT, COLS), F32),
            pltpu.VMEM((CHUNKS, 256, 256), BF16),
            pltpu.VMEM((8, COLS), F32),
            dma((2,)),
            dma((2,)),
            dma((SLOTS,)),
            dma((SLOTS,)),
            dma((n_frames,)),
            dma((n_frames,)),
        ],
        compiler_params=pltpu.CompilerParams(collective_id=0, has_side_effects=True),
    )(raw_movie, shifts, footprints, anchors, block_of.reshape(1, KD), init_traces)
    return traces_z, residual.reshape(2, ROWS, COLS)


def solution(mesh):
    in_specs = (
        P("frames", "slab", None),
        P(None, "frames", "slab", None),
        P("slab", None, None),
        P("slab", None),
        P("slab"),
        P("slab", "frames"),
    )
    out_specs = (P("slab", "frames"), P("frames", "slab", None))
    body = functools.partial(shards, mesh.shape["slab"], mesh.shape["frames"])
    return jax.shard_map(body, mesh=mesh, in_specs=in_specs, out_specs=out_specs, check_vma=False)
```

time: 216 us -> 41.9 us (0.19)
  the two profiles are of different devices: /device:TPU:128 before, /device:TPU:4 now
where the time goes in v1:
time: 41.9 us; the launch traced here: 41.6 us
  Pallas kernels  33.7 us (80%)
  local copies, waits for them, and re-layouts  7.23 us (17%)
  between operations  0.65 us (2%)
    pallas_call x1, Pallas kernels, shards(): pl.pallas_call(functools.partial(kernel, n_slab, n_frames), out_shape=(ja...  33.7 us
    unnamed x10, local copies, waits for them, and re-layouts  7.23 us

profile of v1, /device:TPU:4, one launch (start us, length us, event | category | flops | bytes accessed | tf_op | source)
XLA Modules:
  0.0 41.6 jit_solution(16399685626366685515)
XLA Ops:
  0.6 0.0 copy-start
  0.6 1.4 %copy.8.shift_ref = s32[2,2,2,1]{3,2,1,0:T(2,128)} copy(s32[2,2,2,1]{2,3,1,0:T(1,128)} %param.7) | data formatting | bytes 64 | tf_op args[1]
  2.0 0.0 copy-done
  2.0 0.0 copy-start.1
  2.0 0.7 %copy.10.anchor_ref = s32[32,2]{1,0:T(8,128)} copy(s32[32,2]{0,1:T(2,128)S(1)} %copy-done) | data formatting | bytes 512 | tf_op args[3]
  2.7 0.0 copy-done.1
  2.7 0.7 %copy.11.trace_ref = f32[32,2]{1,0:T(8,128)} copy(f32[32,2]{0,1:T(2,128)S(1)} %copy-done.1) | data formatting | bytes 512 | tf_op args[5]
  3.4 1.6 %copy.9.foot_ref = bf16[32,16,16]{2,1,0:T(8,128)(2,1)} copy(bf16[32,16,16]{0,2,1:T(8,128)(2,1)} %param.8) | data formatting | bytes 32768 | tf_op args[2]
  5.0 33.7 %shard_map.77 = (f32[32,2]{1,0:T(8,128)}, f32[128,128]{1,0:T(8,128)}) custom-call(bf16[2,64,128]{2,1,0:T(8,128)(2,1)} %raw_ref.1, s32[2,2,2,1]{3,2,1,0:T(2,128)} %copy.8.shift_ref, bf16[32,16,16]{2,1,0:T(8,128)(2,1)} %copy.9.foot_ref, s32[32,2]{1,0:T(8,128)} %copy.10.anchor_ref, s32[1,32]{1,0:T(1,128)} %bitcast.3, f32[32,2]{1,0:T(8,128)} %copy.11.trace_ref), custom_call_target="tpu_custom_call" | custom-call | tf_op jit(solution)/shard_map/pallas_call | solution.py:464
  38.8 1.4 %copy.12 = f32[32,2]{0,1:T(2,128)} copy(f32[32,2]{1,0:T(8,128)} %get-tuple-element.6) | data formatting | bytes 512
  40.1 1.5 %copy.14 = f32[2,64,128]{2,1,0:T(8,128)} copy(f32[2,64,128]{2,1,0:T(8,128)} %bitcast.2) | data formatting | bytes 131072
Async XLA Ops:
  0.6 1.4 %copy-start = (s32[32,2]{0,1:T(2,128)S(1)}, s32[32,2]{0,1:T(2,128)}, u32[]{:S(2)}) copy-start(s32[32,2]{0,1:T(2,128)} %param.9) | copy-start | bytes 772
  2.0 0.7 %copy-start.1 = (f32[32,2]{0,1:T(2,128)S(1)}, f32[32,2]{0,1:T(2,128)}, u32[]{:S(2)}) copy-start(f32[32,2]{0,1:T(2,128)} %param.11) | copy-start | bytes 772

commit v2 on v1

--- a/solution.py
+++ b/solution.py
@@ -43,20 +43,45 @@
     return hi, x - hi
 
 
-def place_columns(packed, col, wide_ref):
-    lane_group = iota((TILE, COLS), 1) // TILE
+def column_of(row):
+    square = iota((KD, KD), 0) == iota((KD, KD), 1)
+    return jnp.sum(jnp.where(square, row, 0.0), axis=1, keepdims=True)
+
+
+def tile_map():
+    lane = iota((COLS, 8 * COLS), 1)
+    return jnp.where(
+        iota((COLS, 8 * COLS), 0) == (lane // COLS) * TILE + lane % TILE, 1.0, 0.0
+    ).astype(BF16)
+
+
+def place_columns(flat, col, tiles):
+    stacked = jnp.concatenate([flat[:, 0:COLS], flat[:, COLS:]], axis=0)
+    spread = mm(stacked, tiles)
+    own_group = iota((KD, COLS), 1) // TILE == iota((KD, COLS), 0) % 8
+    rows = [
+        jnp.where(
+            own_group,
+            spread[KD * (i // 8) : KD * (i // 8) + KD, (i % 8) * COLS : (i % 8 + 1) * COLS],
+            0.0,
+        )
+        for i in range(TILE)
+    ]
+    anchor = col + jnp.zeros((KD, COLS), F32)
+    offset = (iota((8, TILE, COLS), 2) - iota((8, TILE, COLS), 1)).astype(F32)
+    out = []
     for g in range(4):
-        rows = packed[g * TILE : (g + 1) * TILE, :]
-        lhs = jnp.concatenate(
-            [jnp.where(lane_group == kk, rows, 0.0).astype(BF16) for kk in range(8)], axis=0
-        )
-        anchor = jnp.broadcast_to(col[8 * g : 8 * g + 8, None, :], (8, TILE, COLS))
-        offset = (iota((8, TILE, COLS), 2) - iota((8, TILE, COLS), 1)).astype(F32)
-        onehot = jnp.where(anchor == offset, 1.0, 0.0).astype(BF16).reshape(COLS, COLS)
-        wide_ref[g * COLS : (g + 1) * COLS, :] = mm(lhs, onehot)
-
-
-def place_rows(row, wide_ref, first, count):
+        lhs = jnp.concatenate([r[8 * g : 8 * g + 8, :] for r in rows], axis=0).astype(BF16)
+        place = jnp.broadcast_to(anchor[8 * g : 8 * g + 8, None, :], (8, TILE, COLS))
+        onehot = jnp.where(place == offset, 1.0, 0.0).astype(BF16).reshape(COLS, COLS)
+        out.append(mm(lhs, onehot))
+    return [
+        jnp.concatenate([out[g][8 * i : 8 * i + 8, :] for g in range(4)], axis=0)
+        for i in range(TILE)
+    ]
+
+
+def place_rows(row, tile_rows, first, count):
     known = {}
     bits = [((row >> b) & 1) == 1 for b in range(6)]
 
@@ -64,9 +89,7 @@
         if y < 0 or y > TILE - 1 + (1 << level) - 1:
             return None
         if level == 0:
-            if (0, y) not in known:
-                known[0, y] = wide_ref[pl.ds(y, KD, stride=TILE), :]
-            return known[0, y]
+            return tile_rows[y]
         if (level, y) not in known:
             moved = at(level - 1, y - (1 << (level - 1)))
             kept = at(level - 1, y)
@@ -96,13 +119,11 @@
     inbox,
     mom_out,
     mom_in,
-    wide,
     image,
     rawx,
     mixed,
     corr,
     band,
-    xrow,
     e1_send,
     e1_recv,
     e2_send,
@@ -135,34 +156,30 @@
     lax.fori_loop(1, HALO + 1, greet_slab, 0)
     lax.fori_loop(1, n_frames, greet_frame, 0)
 
-    foot = foot_ref[...]
-    packed = jnp.zeros((4 * TILE, COLS), F32)
-    for kk in range(8):
-        piece = jnp.concatenate([foot[8 * g + kk] for g in range(4)], axis=0)
-        spread = jnp.where(iota((TILE, COLS), 1) - kk * TILE == iota((TILE, COLS), 0), 1.0, 0.0)
-        packed = packed + mm(piece, spread.astype(BF16))
-    packed = packed.astype(BF16)
-    own_row = (anchor_ref[:, 0:1] - (me * ROWS - RIM)) + jnp.zeros((KD, COLS), jnp.int32)
-    own_col = (anchor_ref[:, 1:2] + jnp.zeros((KD, COLS), jnp.int32)).astype(F32)
-    start = trace_ref[...]
-    t_hi, t_rest = split(start)
-    t_mid, t_lo = split(t_rest)
+    eye = iota((KD, KD), 0) == iota((KD, KD), 1)
+    flat = mm_nt(jnp.where(eye, 1.0, 0.0).astype(BF16), foot_ref[...]).astype(BF16)
+    own_row = column_of((anchor_ref[0:1, :] - (me * ROWS - RIM)).astype(F32))
+    own_col = column_of(anchor_ref[1:2, :].astype(F32))
+    start = [column_of(trace_ref[t : t + 1, :]) for t in range(2)]
     lane = iota((KD, COLS), 1)
-    small = jnp.where(lane == 0, own_row.astype(F32), 0.0)
+    small = jnp.where(lane == 0, own_row, 0.0)
     small = jnp.where(lane == 1, own_col, small)
-    for i, part in enumerate((t_hi, t_mid, t_lo)):
-        for t in range(2):
-            small = jnp.where(lane == 2 + 2 * i + t, part[:, t : t + 1], small)
+    for t in range(2):
+        t_hi, t_rest = split(start[t])
+        t_mid, t_lo = split(t_rest)
+        for i, part in enumerate((t_hi, t_mid, t_lo)):
+            small = jnp.where(lane == 2 + 2 * i + t, part, small)
     for side, patch in ((0, 0), (1, 1)):
         mine = small
         for which in range(2):
             for t in range(2):
-                value = jnp.full((KD, COLS), shift_ref[which, t, patch, 0], jnp.int32).astype(F32)
+                value = jnp.full((KD, COLS), shift_ref[which, t, 0, patch], jnp.int32).astype(F32)
                 mine = jnp.where(lane == 8 + 2 * which + t, value, mine)
         top = 0 if side == 0 else ROWS - 16
         for t in range(2):
             pkt_out[side, 16 * t : 16 * t + 16, :] = raw_ref[t, top : top + 16, :]
-        pkt_out[side, 32:96, :] = packed
+        pkt_out[side, 32:64, :] = flat[:, 0:COLS]
+        pkt_out[side, 64:96, :] = flat[:, COLS:]
         pkt_out[side, 96:128, :] = mine.astype(BF16)
 
     pl.semaphore_wait(barrier, 2 * HALO + n_frames - 1)
@@ -182,13 +199,13 @@
     to_right.start()
 
     image[...] = jnp.zeros(image.shape, BF16)
-    place_columns(packed, own_col, wide)
-    for y, value in enumerate(place_rows(own_row, wide, 0, EXT)):
+    tiles = tile_map()
+    own_int = (own_row + jnp.zeros((KD, COLS), F32)).astype(jnp.int32)
+    for y, value in enumerate(place_rows(own_int, place_columns(flat, own_col, tiles), 0, EXT)):
         if value is not None:
             image[0:KD, y * COLS : (y + 1) * COLS] = value.astype(BF16)
     own = image[0:KD, :]
     gram_own = mm_nt(own, own)
-    eye = iota((KD, KD), 0) == iota((KD, KD), 1)
     norm_sq = jnp.sum(jnp.where(eye, gram_own, 0.0), axis=0, keepdims=True)
     for t in range(2):
         rawx[t * 96 + 16 : t * 96 + 80, :] = raw_ref[t].astype(F32)
@@ -204,9 +221,8 @@
         valid.append(keep)
         info = pkt_in[side, 96:128, :].astype(F32) * keep
         smalls.append(info)
-        place_columns(
-            pkt_in[side, 32:96, :], info[:, 1:2] + jnp.zeros((KD, COLS), F32), wide
-        )
+        theirs = jnp.concatenate([pkt_in[side, 32:64, :], pkt_in[side, 64:96, :]], axis=1)
+        wide = place_columns(theirs, info[:, 1:2], tiles)
         row = (info[:, 0:1] + jnp.zeros((KD, COLS), F32)).astype(jnp.int32)
         first = ROWS if side == 0 else 0
         low = 96 if side == 0 else 32
@@ -226,8 +242,8 @@
         )
         for y0, n in ((-RIM, RIM), (0, 32), (32, 32), (ROWS, RIM)):
             if 0 <= y0 < ROWS:
-                down = jnp.full((n, COLS), shift_ref[0, t, y0 // 32, 0], jnp.int32).astype(F32)
-                across = jnp.full((n, COLS), shift_ref[1, t, y0 // 32, 0], jnp.int32).astype(F32)
+                down = jnp.full((n, COLS), shift_ref[0, t, 0, y0 // 32], jnp.int32).astype(F32)
+                across = jnp.full((n, COLS), shift_ref[1, t, 0, y0 // 32], jnp.int32).astype(F32)
             else:
                 info = smalls[0 if y0 < 0 else 1]
                 down = jnp.broadcast_to(info[0:1, 8 + t : 9 + t], (n, COLS))
@@ -255,7 +271,8 @@
 
     old = [start]
     for info in smalls:
-        old.append(info[:, 2:4] + info[:, 4:6] + info[:, 6:8])
+        exact = info[:, 2:4] + info[:, 4:6] + info[:, 6:8]
+        old.append([exact[:, t : t + 1] for t in range(2)])
     grams = (gram_own, gram_left, gram_right)
     mine = inbox.at[HALO]
     mine[:, 0:32] = gram_left
@@ -264,7 +281,7 @@
     mine[:, 96:128] = jnp.zeros((KD, KD), F32)
     for t in range(2):
         rendered = sum(
-            jnp.sum(gram * x[:, t : t + 1], axis=0, keepdims=True) for gram, x in zip(grams, old)
+            jnp.sum(gram * x[t], axis=0, keepdims=True) for gram, x in zip(grams, old)
         )
         mine[t : t + 1, 96:128] = q[t : t + 1, :] - rendered
     mine[2:3, 96:128] = 1.0 / norm_sq
@@ -301,7 +318,7 @@
         first_rows.append(
             [
                 jnp.sum(
-                    jnp.where(wide_lane - low == wide_row, x[:, t : t + 1], 0.0),
+                    jnp.where(wide_lane - low == wide_row, x[t], 0.0),
                     axis=0,
                     keepdims=True,
                 )
@@ -448,13 +465,7 @@
     square = sums[1:2, :] / count
     spread = square - mean * mean
     z_row = (total3[0:2, :] - mean) / jnp.sqrt(spread + EPSILON)
-    pick = (wide_lane == wide_row) & (wide_lane < KD)
-    cols = [
-        jnp.sum(jnp.where(pick, z_row[t : t + 1, :], 0.0), axis=1, keepdims=True)
-        for t in range(2)
-    ]
-    z_ref[:, 0:1] = cols[0]
-    z_ref[:, 1:2] = cols[1]
+    z_ref[...] = z_row[:, 0:KD]
 
 
 def shards(n_slab, n_frames, raw_movie, shifts, footprints, anchors, block_of, init_traces):
@@ -464,7 +475,7 @@
     traces_z, residual = pl.pallas_call(
         functools.partial(kernel, n_slab, n_frames),
         out_shape=(
-            jax.ShapeDtypeStruct((KD, 2), F32),
+            jax.ShapeDtypeStruct((2, KD), F32),
             jax.ShapeDtypeStruct((2 * ROWS, COLS), F32),
         ),
         in_specs=[vmem, smem, vmem, vmem, vmem, vmem],
@@ -475,13 +486,11 @@
             pltpu.VMEM((SLOTS, KD, COLS), F32),
             pltpu.VMEM((8, COLS), F32),
             pltpu.VMEM((n_frames, 8, COLS), F32),
-            pltpu.VMEM((KD * TILE, COLS), F32),
             pltpu.VMEM((128, EXT * COLS), BF16),
             pltpu.VMEM((192, COLS), F32),
             pltpu.VMEM((192, COLS), F32),
             pltpu.VMEM((8 * EXT, COLS), F32),
             pltpu.VMEM((CHUNKS, 256, 256), BF16),
-            pltpu.VMEM((8, COLS), F32),
             dma((2,)),
             dma((2,)),
             dma((SLOTS,)),
@@ -490,8 +499,15 @@
             dma((n_frames,)),
         ],
         compiler_params=pltpu.CompilerParams(collective_id=0, has_side_effects=True),
-    )(raw_movie, shifts, footprints, anchors, block_of.reshape(1, KD), init_traces)
-    return traces_z, residual.reshape(2, ROWS, COLS)
+    )(
+        raw_movie,
+        shifts.transpose(0, 1, 3, 2),
+        footprints.transpose(1, 2, 0).reshape(TILE * TILE, KD),
+        anchors.T,
+        block_of.reshape(1, KD),
+        init_traces.T,
+    )
+    return traces_z.T, residual.reshape(2, ROWS, COLS)
 
 
 def solution(mesh):

time: 41.9 us -> 37.2 us (0.89)
  local copies, waits for them, and re-layouts: 7.23 us -> 2.69 us
    unnamed x10 -> x4, local copies, waits for them, and re-layouts: 7.23 us -> 2.69 us
where the time goes in v2:
time: 37.2 us; the launch traced here: 37.1 us
  Pallas kernels  33.7 us (91%)
  local copies, waits for them, and re-layouts  2.69 us (7%)
  between operations  0.65 us (2%)
    pallas_call x1, Pallas kernels, shards(): pl.pallas_call(functools.partial(kernel, n_slab, n_frames), out_shape=(ja...  33.7 us
    unnamed x4, local copies, waits for them, and re-layouts  2.69 us

profile of v2, /device:TPU:4, one launch (start us, length us, event | category | flops | bytes accessed | tf_op | source)
XLA Modules:
  0.0 37.1 jit_solution(9357664878030427250)
XLA Ops:
  0.6 33.7 %shard_map.77 = (f32[2,32]{1,0:T(2,128)}, f32[128,128]{1,0:T(8,128)}) custom-call(bf16[2,64,128]{2,1,0:T(8,128)(2,1)} %raw_ref.1, s32[2,2,1,2]{3,2,1,0:T(1,128)} %bitcast.13, bf16[256,32]{1,0:T(8,128)(2,1)} %bitcast.11, s32[2,32]{1,0:T(2,128)} %bitcast.14, s32[1,32]{1,0:T(1,128)} %bitcast.17, f32[2,32]{1,0:T(2,128)} %bitcast.15), custom_call_target="tpu_custom_call" | custom-call | tf_op jit(solution)/shard_map/pallas_call | solution.py:475
  34.4 0.0 copy-start
  34.4 0.7 %copy-done = f32[2,32]{1,0:T(2,128)S(1)} copy-done((f32[2,32]{1,0:T(2,128)S(1)}, f32[2,32]{1,0:T(2,128)}, u32[]{:S(2)}) %copy-start) | copy-done | bytes 280
  35.0 0.6 %copy.11 = f32[32,2]{0,1:T(2,128)} copy(f32[32,2]{0,1:T(2,128)S(1)} %bitcast.16) | data formatting | bytes 512
  35.6 1.5 %copy.12 = f32[2,64,128]{2,1,0:T(8,128)} copy(f32[2,64,128]{2,1,0:T(8,128)} %bitcast.12) | data formatting | bytes 131072
Async XLA Ops:
  34.4 0.7 %copy-start = (f32[2,32]{1,0:T(2,128)S(1)}, f32[2,32]{1,0:T(2,128)}, u32[]{:S(2)}) copy-start(f32[2,32]{1,0:T(2,128)} %get-tuple-element.4) | copy-start | bytes 772

commit v3 on v2

--- a/solution.py
+++ b/solution.py
@@ -116,7 +116,8 @@
     res_ref,
     pkt_out,
     pkt_in,
-    inbox,
+    early,
+    late,
     mom_out,
     mom_in,
     image,
@@ -124,10 +125,13 @@
     mixed,
     corr,
     band,
+    square,
     e1_send,
     e1_recv,
-    e2_send,
-    e2_recv,
+    early_send,
+    early_recv,
+    late_send,
+    late_recv,
     e3_send,
     e3_recv,
 ):
@@ -145,7 +149,10 @@
     def greet_slab(i, carry):
         for sign in (1, -1):
             pl.semaphore_signal(
-                barrier, 1, device_id={"slab": slab_at(sign * i)}, device_id_type=MESH
+                barrier,
+                1,
+                device_id={"slab": slab_at(sign * (HALO + 1 - i))},
+                device_id_type=MESH,
             )
         return carry
 
@@ -207,8 +214,85 @@
     own = image[0:KD, :]
     gram_own = mm_nt(own, own)
     norm_sq = jnp.sum(jnp.where(eye, gram_own, 0.0), axis=0, keepdims=True)
+    def message(ref, send_sem, recv_sem, offset):
+        slot = HALO - offset
+        return pltpu.make_async_remote_copy(
+            src_ref=ref.at[HALO],
+            dst_ref=ref.at[slot],
+            send_sem=send_sem.at[slot],
+            recv_sem=recv_sem.at[slot],
+            device_id={"slab": slab_at(offset)},
+            device_id_type=MESH,
+        )
+
+    def send(ref, send_sem, recv_sem, i, carry):
+        message(ref, send_sem, recv_sem, HALO + 1 - i).start()
+        message(ref, send_sem, recv_sem, i - HALO - 1).start()
+        return carry
+
+    def arrive(ref, send_sem, recv_sem, i, carry):
+        message(ref, send_sem, recv_sem, i).wait()
+        message(ref, send_sem, recv_sem, -i).wait()
+        return carry
+
+    early_set = (early, early_send, early_recv)
+    late_set = (late, late_send, late_recv)
+
+    def compact(gram):
+        square[:, 0:KD] = gram
+        total = square[0:8, :]
+        for g in range(1, 4):
+            total = total + pltpu.roll(square[8 * g : 8 * g + 8, :], KD * g, 1)
+        return total
+
+    square[...] = jnp.zeros((KD, COLS), F32)
+    early[HALO, 0:8, :] = compact(gram_own)
+    early[HALO, 8:16, :] = jnp.zeros((8, COLS), F32)
+    early[HALO, 8:9, 0:KD] = 1.0 / norm_sq
+    early[HALO, 9:10, 0:KD] = block_ref[...].astype(F32)
+    lax.fori_loop(1, HALO + 1, functools.partial(send, *early_set), 0)
+
+    def mix(t, low, high):
+        at = t * 96 + low + 4
+        mixed[t * 96 + low : t * 96 + high, :] = (
+            0.75 * rawx[at : at + high - low, :] + 0.25 * rawx[at + 1 : at + 1 + high - low, :]
+        )
+
+    def correct(t, y0, n, down, across, keep):
+        picked = jnp.zeros((n, COLS), F32)
+        for a in range(-3, 4):
+            at = t * 96 + y0 + 12 + a
+            picked = jnp.where(down == a, mixed[at : at + n, :], picked)
+        place = iota((n, COLS), 1)
+        moved = jnp.zeros((n, COLS), F32)
+        for c in range(-3, 4):
+            turned = picked if c == 0 else pltpu.roll(picked, (-c) % COLS, 1)
+            within = (place + c >= 0) & (place + c < COLS)
+            moved = jnp.where((across == c) & within, turned, moved)
+        moved = moved.astype(BF16).astype(F32)
+        if keep is not None:
+            moved = moved * keep
+        at = t * EXT + y0 + RIM
+        corr[at : at + n, :] = moved
+
+    def correct_own(t, y0, n):
+        down, across = (
+            jnp.full((n, COLS), shift_ref[which, t, 0, y0 // 32], jnp.int32).astype(F32)
+            for which in range(2)
+        )
+        correct(t, y0, n, down, across, None)
+
+    def frame_rows(low, high):
+        rows = [corr[pl.ds(y, 8, stride=EXT), :] for y in range(low, high)]
+        return jnp.concatenate(rows, axis=1).astype(BF16)
+
+    corr[2 * EXT :, :] = jnp.zeros((6 * EXT, COLS), F32)
     for t in range(2):
         rawx[t * 96 + 16 : t * 96 + 80, :] = raw_ref[t].astype(F32)
+        mix(t, 12, 75)
+        correct_own(t, 8, 24)
+        correct_own(t, 32, 24)
+    q_inner = mm_nt(frame_rows(16, ROWS), image[0:KD, 16 * COLS : ROWS * COLS])
 
     to_left.wait()
     to_right.wait()
@@ -237,78 +321,34 @@
     gram_right = mm_nt(image[32:64, ROWS * COLS :], image[0:KD, ROWS * COLS :])
 
     for t in range(2):
-        mixed[t * 96 : t * 96 + 88, :] = (
-            0.75 * rawx[t * 96 + 4 : t * 96 + 92, :] + 0.25 * rawx[t * 96 + 5 : t * 96 + 93, :]
-        )
-        for y0, n in ((-RIM, RIM), (0, 32), (32, 32), (ROWS, RIM)):
-            if 0 <= y0 < ROWS:
-                down = jnp.full((n, COLS), shift_ref[0, t, 0, y0 // 32], jnp.int32).astype(F32)
-                across = jnp.full((n, COLS), shift_ref[1, t, 0, y0 // 32], jnp.int32).astype(F32)
-            else:
-                info = smalls[0 if y0 < 0 else 1]
-                down = jnp.broadcast_to(info[0:1, 8 + t : 9 + t], (n, COLS))
-                across = jnp.broadcast_to(info[0:1, 10 + t : 11 + t], (n, COLS))
-            picked = jnp.zeros((n, COLS), F32)
-            for a in range(-3, 4):
-                at = t * 96 + y0 + 12 + a
-                picked = jnp.where(down == a, mixed[at : at + n, :], picked)
-            place = iota((n, COLS), 1)
-            moved = jnp.zeros((n, COLS), F32)
-            for c in range(-3, 4):
-                turned = picked if c == 0 else pltpu.roll(picked, (-c) % COLS, 1)
-                within = (place + c >= 0) & (place + c < COLS)
-                moved = jnp.where((across == c) & within, turned, moved)
-            moved = moved.astype(BF16).astype(F32)
-            if y0 < 0:
-                moved = moved * valid[0]
-            if y0 >= ROWS:
-                moved = moved * valid[1]
-            at = t * EXT + y0 + RIM
-            corr[at : at + n, :] = moved
-    corr[2 * EXT :, :] = jnp.zeros((6 * EXT, COLS), F32)
-    frames_rows = jnp.concatenate([corr[pl.ds(y, 8, stride=EXT), :] for y in range(EXT)], axis=1)
-    q = mm_nt(frames_rows.astype(BF16), image[0:KD, :])
+        mix(t, 0, 12)
+        mix(t, 75, 88)
+        correct_own(t, 0, RIM)
+        correct_own(t, ROWS - RIM, RIM)
+        for side, y0 in ((0, -RIM), (1, ROWS)):
+            info = smalls[side]
+            down = jnp.broadcast_to(info[0:1, 8 + t : 9 + t], (RIM, COLS))
+            across = jnp.broadcast_to(info[0:1, 10 + t : 11 + t], (RIM, COLS))
+            correct(t, y0, RIM, down, across, valid[side])
+    q = (
+        q_inner
+        + mm_nt(frame_rows(0, 16), image[0:KD, 0 : 16 * COLS])
+        + mm_nt(frame_rows(ROWS, EXT), image[0:KD, ROWS * COLS :])
+    )
 
     old = [start]
     for info in smalls:
         exact = info[:, 2:4] + info[:, 4:6] + info[:, 6:8]
         old.append([exact[:, t : t + 1] for t in range(2)])
     grams = (gram_own, gram_left, gram_right)
-    mine = inbox.at[HALO]
-    mine[:, 0:32] = gram_left
-    mine[:, 32:64] = gram_own
-    mine[:, 64:96] = gram_right
-    mine[:, 96:128] = jnp.zeros((KD, KD), F32)
+    late[HALO, 0:8, :] = compact(gram_left)
+    late[HALO, 8:16, :] = jnp.zeros((8, COLS), F32)
     for t in range(2):
         rendered = sum(
             jnp.sum(gram * x[t], axis=0, keepdims=True) for gram, x in zip(grams, old)
         )
-        mine[t : t + 1, 96:128] = q[t : t + 1, :] - rendered
-    mine[2:3, 96:128] = 1.0 / norm_sq
-    mine[3:4, 96:128] = block_ref[...].astype(F32)
-
-    def message(offset):
-        slot = HALO - offset
-        return pltpu.make_async_remote_copy(
-            src_ref=inbox.at[HALO],
-            dst_ref=inbox.at[slot],
-            send_sem=e2_send.at[slot],
-            recv_sem=e2_recv.at[slot],
-            device_id={"slab": slab_at(offset)},
-            device_id_type=MESH,
-        )
-
-    def send(i, carry):
-        message(i).start()
-        message(-i).start()
-        return carry
-
-    def arrive(i, carry):
-        message(i).wait()
-        message(-i).wait()
-        return carry
-
-    lax.fori_loop(1, HALO + 1, send, 0)
+        late[HALO, 8 + t : 9 + t, 0:KD] = q[t : t + 1, :] - rendered
+    lax.fori_loop(1, HALO + 1, functools.partial(send, *late_set), 0)
 
     lanes8 = iota((8, COLS), 1)
     wide_lane = iota((KD, COLS), 1)
@@ -332,61 +372,65 @@
 
     own_x, left_x, right_x = (rows_of(pair) for pair in first_rows)
 
-    lax.fori_loop(1, HALO + 1, arrive, 0)
-
-    def block_of_slot(slot, which, lane_chunk):
-        value = inbox[slot]
-        turn = (32 * (lane_chunk - which)) % COLS
-        return value if turn == 0 else pltpu.roll(value, turn, 1)
-
-    lane_chunk = wide_lane // 32
-    scal = []
+    lax.fori_loop(1, HALO + 1, functools.partial(arrive, *early_set), 0)
+    lax.fori_loop(1, HALO + 1, functools.partial(arrive, *late_set), 0)
+
+    group8 = lanes8 // KD
+
+    def turned(value, turn):
+        return value if turn % COLS == 0 else pltpu.roll(value, turn % COLS, 1)
+
+    def keep_of(slot):
+        where = me + (slot - HALO)
+        return jnp.where((where >= 0) & (where < n_slab), 1.0, 0.0).astype(F32)
+
+    def spread(tile, i):
+        parts = [jnp.where(group8 == i, turned(tile, KD * (i - g)), 0.0) for g in range(4)]
+        return jnp.concatenate(parts, axis=0)
+
+    zero32 = jnp.zeros((KD, COLS), F32)
+    zero8 = jnp.zeros((8, COLS), F32)
+    state, gains = [], []
+    before = zero32
     for m in range(CHUNKS):
-        keeps = []
+        p_rows, gain_rows, diag, links = zero8, zero8, [], []
         for i in range(4):
             slot = 4 * m + i
-            if slot >= SLOTS:
-                keeps.append(None)
-                continue
-            where = me + (slot - HALO)
-            keeps.append(jnp.where((where >= 0) & (where < n_slab), 1.0, 0.0).astype(F32))
-        tops = jnp.zeros((8, COLS), F32)
+            if slot < SLOTS:
+                keep = keep_of(slot)
+                rows = jnp.where(group8 == i, turned(late[slot, 8:16, :], KD * i), 0.0)
+                p_rows = p_rows + rows * keep
+                rows = jnp.where(group8 == i, turned(early[slot, 8:16, :], KD * i), 0.0)
+                gain_rows = gain_rows + rows * keep
+                diag.append(spread(early[slot, 0:8, :] * keep, i))
+            else:
+                diag.append(zero32)
+            after = slot + 1
+            if after < SLOTS:
+                links.append(spread(late[after, 0:8, :] * keep_of(after), (i + 1) % 4))
+            else:
+                links.append(zero32)
+        state.append(p_rows)
+        gains.append(
+            [jnp.where(gain_rows[1:2, :] == float(b), gain_rows[0:1, :], 0.0) for b in range(BLOCKS)]
+        )
+        upper = jnp.concatenate(links, axis=0)
+        lower = upper.T
+        corner = lower[0:KD, :]
+        blocks = []
         for i in range(4):
-            if keeps[i] is None:
-                continue
-            top = inbox[4 * m + i, 0:8, :]
-            turn = (32 * (i - 3)) % COLS
-            top = top if turn == 0 else pltpu.roll(top, turn, 1)
-            tops = tops + jnp.where(lanes8 // 32 == i, top * keeps[i], 0.0)
-        scal.append(tops)
-        parts = []
-        for rows in range(8):
-            terms = []
-            if rows < 4:
-                terms = [(rows, 1), (rows + 1, 0), (rows - 1, 2)]
-            elif rows == 4:
-                terms = [(3, 2)]
-            elif rows == 7:
-                terms = [(0, 0)]
-            total = jnp.zeros((KD, COLS), F32)
-            for i, which in terms:
-                if 0 <= i < 4 and keeps[i] is not None:
-                    value = block_of_slot(4 * m + i, which, i) * keeps[i]
-                    total = total + jnp.where(lane_chunk == i, value, 0.0)
-            parts.append(total)
-        for rows, total in enumerate(parts):
-            hi, lo = split(total)
-            band[m, rows * KD : (rows + 1) * KD, 0:COLS] = hi.astype(BF16)
-            band[m, rows * KD : (rows + 1) * KD, COLS:] = lo.astype(BF16)
-
-    state = list(scal)
-    gains = [
-        [
-            jnp.where(tops[3:4, :] == float(b), tops[2:3, :], 0.0)
-            for b in range(BLOCKS)
-        ]
-        for tops in scal
-    ]
+            value = diag[i]
+            if i < 3:
+                value = value + links[i]
+            if i > 0:
+                value = value + lower[KD * i : KD * i + KD, :]
+            blocks.append(value)
+        for at, value in ((0, blocks[0]), (1, blocks[1]), (2, blocks[2]), (3, blocks[3]), (4, corner), (5, zero32), (6, zero32), (7, before)):
+            hi, lo = split(value)
+            band[m, at * KD : (at + 1) * KD, 0:COLS] = hi.astype(BF16)
+            band[m, at * KD : (at + 1) * KD, COLS:] = lo.astype(BF16)
+        before = links[3]
+
     total2 = jnp.where(lanes8 >= 96, left_x, 0.0)
     total3 = own_x + right_x
     for step in range(1, STEPS + 1):
@@ -468,6 +512,11 @@
     z_ref[...] = z_row[:, 0:KD]
 
 
+def hand_on(z_ref, res_ref, z_out, res_out):
+    z_out[...] = z_ref[...]
+    res_out[...] = res_ref[...]
+
+
 def shards(n_slab, n_frames, raw_movie, shifts, footprints, anchors, block_of, init_traces):
     vmem = pl.BlockSpec(memory_space=pltpu.VMEM)
     smem = pl.BlockSpec(memory_space=pltpu.SMEM)
@@ -483,7 +532,8 @@
         scratch_shapes=[
             pltpu.VMEM((2, 128, COLS), BF16),
             pltpu.VMEM((2, 128, COLS), BF16),
-            pltpu.VMEM((SLOTS, KD, COLS), F32),
+            pltpu.VMEM((SLOTS, 16, COLS), F32),
+            pltpu.VMEM((SLOTS, 16, COLS), F32),
             pltpu.VMEM((8, COLS), F32),
             pltpu.VMEM((n_frames, 8, COLS), F32),
             pltpu.VMEM((128, EXT * COLS), BF16),
@@ -491,8 +541,11 @@
             pltpu.VMEM((192, COLS), F32),
             pltpu.VMEM((8 * EXT, COLS), F32),
             pltpu.VMEM((CHUNKS, 256, 256), BF16),
+            pltpu.VMEM((KD, COLS), F32),
             dma((2,)),
             dma((2,)),
+            dma((SLOTS,)),
+            dma((SLOTS,)),
             dma((SLOTS,)),
             dma((SLOTS,)),
             dma((n_frames,)),
@@ -507,6 +560,13 @@
         block_of.reshape(1, KD),
         init_traces.T,
     )
+    traces_z, residual = pl.pallas_call(
+        hand_on,
+        out_shape=(
+            jax.ShapeDtypeStruct((2, KD), F32),
+            jax.ShapeDtypeStruct((2 * ROWS, COLS), F32),
+        ),
+    )(traces_z, residual)
     return traces_z.T, residual.reshape(2, ROWS, COLS)
 
 

time: 37.2 us -> 33.8 us (0.909)
  the two profiles are of different devices: /device:TPU:4 before, /device:TPU:1 now
where the time goes in v3:
time: 33.8 us; the launch traced here: 33.6 us
  Pallas kernels  33 us (98%)
  between operations  0.64 us (2%)
    pallas_call x1, Pallas kernels, shards(): pl.pallas_call(functools.partial(kernel, n_slab, n_frames), out_shape=(ja...  31.5 us
    pallas_call x1, Pallas kernels, shards(): pl.pallas_call(hand_on, out_shape=(jax.ShapeDtypeStruct((2, KD), F32), ja...  1.48 us

profile of v3, /device:TPU:1, one launch (start us, length us, event | category | flops | bytes accessed | tf_op | source)
XLA Modules:
  0.0 33.6 jit_solution(17284691766275502052)
XLA Ops:
  0.6 31.5 %shard_map.77 = (f32[2,32]{1,0:T(2,128)}, f32[128,128]{1,0:T(8,128)}) custom-call(bf16[2,64,128]{2,1,0:T(8,128)(2,1)} %raw_ref.1, s32[2,2,1,2]{3,2,1,0:T(1,128)} %bitcast.12, bf16[256,32]{1,0:T(8,128)(2,1)} %bitcast.11, s32[2,32]{1,0:T(2,128)} %bitcast.13, s32[1,32]{1,0:T(1,128)} %bitcast.15, f32[2,32]{1,0:T(2,128)} %bitcast.14), custom_call_target="tpu_custom_call" | custom-call | tf_op jit(solution)/shard_map/pallas_call | solution.py:524
  32.2 1.5 %shard_map.78 = (f32[2,32]{1,0:T(2,128)}, f32[128,128]{1,0:T(8,128)}) custom-call(f32[2,32]{1,0:T(2,128)} %get-tuple-element.6.z_ref, f32[128,128]{1,0:T(8,128)} %get-tuple-element.7.res_ref), custom_call_target="tpu_custom_call" | custom-call | tf_op jit(solution)/shard_map/pallas_call | solution.py:563

commit v4 on v3

--- a/solution.py
+++ b/solution.py
@@ -217,8 +217,8 @@
     def message(ref, send_sem, recv_sem, offset):
         slot = HALO - offset
         return pltpu.make_async_remote_copy(
-            src_ref=ref.at[HALO],
-            dst_ref=ref.at[slot],
+            src_ref=ref.at[HALO, 0:10],
+            dst_ref=ref.at[slot, 0:10],
             send_sem=send_sem.at[slot],
             recv_sem=recv_sem.at[slot],
             device_id={"slab": slab_at(offset)},
@@ -512,9 +512,15 @@
     z_ref[...] = z_row[:, 0:KD]
 
 
-def hand_on(z_ref, res_ref, z_out, res_out):
-    z_out[...] = z_ref[...]
-    res_out[...] = res_ref[...]
+def hand_on(z_ref, res_ref, z_out, res_out, sems):
+    copies = [
+        pltpu.make_async_copy(res_ref, res_out, sems.at[0]),
+        pltpu.make_async_copy(z_ref, z_out, sems.at[1]),
+    ]
+    for copy in copies:
+        copy.start()
+    for copy in copies:
+        copy.wait()
 
 
 def shards(n_slab, n_frames, raw_movie, shifts, footprints, anchors, block_of, init_traces):
@@ -524,8 +530,8 @@
     traces_z, residual = pl.pallas_call(
         functools.partial(kernel, n_slab, n_frames),
         out_shape=(
-            jax.ShapeDtypeStruct((2, KD), F32),
-            jax.ShapeDtypeStruct((2 * ROWS, COLS), F32),
+            pltpu.VMEM((2, KD), F32),
+            pltpu.VMEM((2 * ROWS, COLS), F32),
         ),
         in_specs=[vmem, smem, vmem, vmem, vmem, vmem],
         out_specs=(vmem, vmem),
@@ -560,12 +566,17 @@
         block_of.reshape(1, KD),
         init_traces.T,
     )
+    traces_z = pltpu.with_memory_space_constraint(traces_z, pltpu.VMEM)
+    residual = pltpu.with_memory_space_constraint(residual, pltpu.VMEM)
     traces_z, residual = pl.pallas_call(
         hand_on,
         out_shape=(
             jax.ShapeDtypeStruct((2, KD), F32),
             jax.ShapeDtypeStruct((2 * ROWS, COLS), F32),
         ),
+        in_specs=[pl.BlockSpec(memory_space=pltpu.VMEM)] * 2,
+        out_specs=(pl.BlockSpec(memory_space=pltpu.HBM),) * 2,
+        scratch_shapes=[dma((2,))],
     )(traces_z, residual)
     return traces_z.T, residual.reshape(2, ROWS, COLS)
 

time: 33.8 us -> 31.5 us (0.932)
  Pallas kernels: 33 us -> 30.7 us
    pallas_call x1, Pallas kernels: 31.5 us -> 30 us  [shards(): pl.pallas_call(functools.partial(kernel, n_slab, n_frames), out_shape=(pl...]
    pallas_call x1, Pallas kernels: 1.48 us -> 0.65 us  [shards(): pl.pallas_call(hand_on, out_shape=(jax.ShapeDtypeStruct((2, KD), F32), ja...]
where the time goes in v4:
time: 31.5 us; the launch traced here: 31.3 us
  Pallas kernels  30.7 us (97%)
  between operations  0.64 us (2%)
    pallas_call x1, Pallas kernels, shards(): pl.pallas_call(functools.partial(kernel, n_slab, n_frames), out_shape=(pl...  30 us
    pallas_call x1, Pallas kernels, shards(): pl.pallas_call(hand_on, out_shape=(jax.ShapeDtypeStruct((2, KD), F32), ja...  0.65 us

profile of v4, /device:TPU:1, one launch (start us, length us, event | category | flops | bytes accessed | tf_op | source)
XLA Modules:
  0.0 31.3 jit_solution(860715303072282680)
XLA Ops:
  0.6 30.0 %shard_map.77 = (f32[2,32]{1,0:T(2,128)S(1)}, f32[128,128]{1,0:T(8,128)S(1)}) custom-call(bf16[2,64,128]{2,1,0:T(8,128)(2,1)} %raw_ref.1, s32[2,2,1,2]{3,2,1,0:T(1,128)} %bitcast.12, bf16[256,32]{1,0:T(8,128)(2,1)} %bitcast.11, s32[2,32]{1,0:T(2,128)} %bitcast.13, s32[1,32]{1,0:T(1,128)} %bitcast.15, f32[2,32]{1,0:T(2,128)} %bitcast.14), custom_call_target="tpu_custom_call" | custom-call | tf_op jit(solution)/shard_map/pallas_call | solution.py:530
  30.7 0.7 %shard_map.78 = (f32[2,32]{1,0:T(2,128)}, f32[128,128]{1,0:T(8,128)}) custom-call(f32[2,32]{1,0:T(2,128)S(1)} %get-tuple-element.6.z_ref, f32[128,128]{1,0:T(8,128)S(1)} %get-tuple-element.7.res_ref), custom_call_target="tpu_custom_call" | custom-call | tf_op jit(solution)/shard_map/pallas_call | solution.py:571

commit v5 on v4

--- a/solution.py
+++ b/solution.py
@@ -106,14 +106,21 @@
 def kernel(
     n_slab,
     n_frames,
+    raw_in,
+    shift_in,
+    foot_in,
+    anchor_in,
+    block_in,
+    trace_in,
+    z_ref,
+    res_ref,
     raw_ref,
     shift_ref,
     foot_ref,
     anchor_ref,
     block_ref,
     trace_ref,
-    z_ref,
-    res_ref,
+    fetched,
     pkt_out,
     pkt_in,
     early,
@@ -162,6 +169,24 @@
 
     lax.fori_loop(1, HALO + 1, greet_slab, 0)
     lax.fori_loop(1, n_frames, greet_frame, 0)
+
+    fetches = [
+        pltpu.make_async_copy(source, target, fetched.at[i])
+        for i, (source, target) in enumerate(
+            (
+                (foot_in, foot_ref),
+                (anchor_in, anchor_ref),
+                (trace_in, trace_ref),
+                (raw_in, raw_ref),
+                (shift_in, shift_ref),
+                (block_in, block_ref),
+            )
+        )
+    ]
+    for fetch in fetches:
+        fetch.start()
+    for fetch in fetches:
+        fetch.wait()
 
     eye = iota((KD, KD), 0) == iota((KD, KD), 1)
     flat = mm_nt(jnp.where(eye, 1.0, 0.0).astype(BF16), foot_ref[...]).astype(BF16)
@@ -462,7 +487,6 @@
     final = jnp.where(own_lane & two_rows, total3, 0.0)
     mom_out[0:1, :] = jnp.sum(final, axis=0, keepdims=True)
     mom_out[1:2, :] = jnp.sum(final * final, axis=0, keepdims=True)
-    mom_out[2:8, :] = jnp.zeros((6, COLS), F32)
 
     def moments(i):
         return pltpu.make_async_remote_copy(
@@ -525,7 +549,6 @@
 
 def shards(n_slab, n_frames, raw_movie, shifts, footprints, anchors, block_of, init_traces):
     vmem = pl.BlockSpec(memory_space=pltpu.VMEM)
-    smem = pl.BlockSpec(memory_space=pltpu.SMEM)
     dma = pltpu.SemaphoreType.DMA
     traces_z, residual = pl.pallas_call(
         functools.partial(kernel, n_slab, n_frames),
@@ -533,15 +556,22 @@
             pltpu.VMEM((2, KD), F32),
             pltpu.VMEM((2 * ROWS, COLS), F32),
         ),
-        in_specs=[vmem, smem, vmem, vmem, vmem, vmem],
+        in_specs=[pl.BlockSpec(memory_space=pl.ANY)] * 6,
         out_specs=(vmem, vmem),
         scratch_shapes=[
+            pltpu.VMEM((2, ROWS, COLS), BF16),
+            pltpu.SMEM((2, 2, 1, 2), jnp.int32),
+            pltpu.VMEM((TILE * TILE, KD), BF16),
+            pltpu.VMEM((2, KD), jnp.int32),
+            pltpu.VMEM((1, KD), jnp.int32),
+            pltpu.VMEM((2, KD), F32),
+            dma((6,)),
             pltpu.VMEM((2, 128, COLS), BF16),
             pltpu.VMEM((2, 128, COLS), BF16),
             pltpu.VMEM((SLOTS, 16, COLS), F32),
             pltpu.VMEM((SLOTS, 16, COLS), F32),
-            pltpu.VMEM((8, COLS), F32),
-            pltpu.VMEM((n_frames, 8, COLS), F32),
+            pltpu.VMEM((2, COLS), F32),
+            pltpu.VMEM((n_frames, 2, COLS), F32),
             pltpu.VMEM((128, EXT * COLS), BF16),
             pltpu.VMEM((192, COLS), F32),
             pltpu.VMEM((192, COLS), F32),

time: 31.5 us -> 30.6 us (0.971)
  Pallas kernels: 30.7 us -> 29.9 us
    pallas_call x1, Pallas kernels: 30 us -> 29.2 us  [shards(): pl.pallas_call(functools.partial(kernel, n_slab, n_frames), out_shape=(pl...]
where the time goes in v5:
time: 30.6 us; the launch traced here: 30.5 us
  Pallas kernels  29.9 us (98%)
  between operations  0.64 us (2%)
    pallas_call x1, Pallas kernels, shards(): pl.pallas_call(functools.partial(kernel, n_slab, n_frames), out_shape=(pl...  29.2 us
    pallas_call x1, Pallas kernels, shards(): pl.pallas_call(hand_on, out_shape=(jax.ShapeDtypeStruct((2, KD), F32), ja...  0.65 us

profile of v5, /device:TPU:1, one launch (start us, length us, event | category | flops | bytes accessed | tf_op | source)
XLA Modules:
  0.0 30.5 jit_solution(980090380748561455)
XLA Ops:
  0.6 29.2 %shard_map.77 = (f32[2,32]{1,0:T(2,128)S(1)}, f32[128,128]{1,0:T(8,128)S(1)}) custom-call(bf16[2,64,128]{2,1,0:T(8,128)(2,1)} %raw_in.1, s32[2,2,1,2]{3,2,1,0:T(1,128)} %bitcast.12, bf16[256,32]{1,0:T(8,128)(2,1)} %bitcast.11, s32[2,32]{1,0:T(2,128)} %bitcast.13, s32[1,32]{1,0:T(1,128)} %bitcast.15, f32[2,32]{1,0:T(2,128)} %bitcast.14), custom_call_target="tpu_custom_call" | custom-call | tf_op jit(solution)/shard_map/pallas_call | solution.py:553
  29.8 0.7 %shard_map.78 = (f32[2,32]{1,0:T(2,128)}, f32[128,128]{1,0:T(8,128)}) custom-call(f32[2,32]{1,0:T(2,128)S(1)} %get-tuple-element.6.z_ref, f32[128,128]{1,0:T(8,128)S(1)} %get-tuple-element.7.res_ref), custom_call_target="tpu_custom_call" | custom-call | tf_op jit(solution)/shard_map/pallas_call | solution.py:601

commit v6 on v5

--- a/solution.py
+++ b/solution.py
@@ -244,8 +244,8 @@
         return pltpu.make_async_remote_copy(
             src_ref=ref.at[HALO, 0:10],
             dst_ref=ref.at[slot, 0:10],
-            send_sem=send_sem.at[slot],
-            recv_sem=recv_sem.at[slot],
+            send_sem=send_sem,
+            recv_sem=recv_sem,
             device_id={"slab": slab_at(offset)},
             device_id_type=MESH,
         )
@@ -255,10 +255,9 @@
         message(ref, send_sem, recv_sem, i - HALO - 1).start()
         return carry
 
-    def arrive(ref, send_sem, recv_sem, i, carry):
-        message(ref, send_sem, recv_sem, i).wait()
-        message(ref, send_sem, recv_sem, -i).wait()
-        return carry
+    def arrived(ref, sem):
+        whole = ref.at[0 : 2 * HALO, 0:10]
+        pltpu.make_async_copy(whole, whole, sem).wait()
 
     early_set = (early, early_send, early_recv)
     late_set = (late, late_send, late_recv)
@@ -397,8 +396,8 @@
 
     own_x, left_x, right_x = (rows_of(pair) for pair in first_rows)
 
-    lax.fori_loop(1, HALO + 1, functools.partial(arrive, *early_set), 0)
-    lax.fori_loop(1, HALO + 1, functools.partial(arrive, *late_set), 0)
+    arrived(early, early_recv)
+    arrived(late, late_recv)
 
     group8 = lanes8 // KD
 
@@ -492,18 +491,14 @@
         return pltpu.make_async_remote_copy(
             src_ref=mom_out,
             dst_ref=mom_in.at[n_frames - i],
-            send_sem=e3_send.at[n_frames - i],
-            recv_sem=e3_recv.at[n_frames - i],
+            send_sem=e3_send,
+            recv_sem=e3_recv,
             device_id={"frames": frame_at(i)},
             device_id_type=MESH,
         )
 
     def send_moments(i, carry):
         moments(i).start()
-        return carry
-
-    def arrive_moments(i, carry):
-        moments(i).wait()
         return carry
 
     lax.fori_loop(1, n_frames, send_moments, 0)
@@ -524,7 +519,11 @@
             res_ref[pl.ds(y, 2, stride=ROWS), :] = rows[0:2, :]
             y += 1
 
-    lax.fori_loop(1, n_frames, arrive_moments, 0)
+    arrived(early, early_send)
+    arrived(late, late_send)
+    others = mom_in.at[1:n_frames]
+    pltpu.make_async_copy(others, others, e3_send).wait()
+    pltpu.make_async_copy(others, others, e3_recv).wait()
     sums = mom_out[...]
     for i in range(1, n_frames):
         sums = sums + mom_in[i]
@@ -580,12 +579,12 @@
             pltpu.VMEM((KD, COLS), F32),
             dma((2,)),
             dma((2,)),
-            dma((SLOTS,)),
-            dma((SLOTS,)),
-            dma((SLOTS,)),
-            dma((SLOTS,)),
-            dma((n_frames,)),
-            dma((n_frames,)),
+            dma,
+            dma,
+            dma,
+            dma,
+            dma,
+            dma,
         ],
         compiler_params=pltpu.CompilerParams(collective_id=0, has_side_effects=True),
     )(

time: 30.6 us -> 29.5 us (0.964)
  Pallas kernels: 29.9 us -> 28.7 us
    pallas_call x1, Pallas kernels: 29.2 us -> 28.1 us  [shards(): pl.pallas_call(functools.partial(kernel, n_slab, n_frames), out_shape=(pl...]
where the time goes in v6:
time: 29.5 us; the launch traced here: 29.4 us
  Pallas kernels  28.7 us (97%)
  between operations  0.64 us (2%)
    pallas_call x1, Pallas kernels, shards(): pl.pallas_call(functools.partial(kernel, n_slab, n_frames), out_shape=(pl...  28.1 us
    pallas_call x1, Pallas kernels, shards(): pl.pallas_call(hand_on, out_shape=(jax.ShapeDtypeStruct((2, KD), F32), ja...  0.65 us

profile of v6, /device:TPU:1, one launch (start us, length us, event | category | flops | bytes accessed | tf_op | source)
XLA Modules:
  0.0 29.4 jit_solution(6425519226017249231)
XLA Ops:
  0.6 28.1 %shard_map.77 = (f32[2,32]{1,0:T(2,128)S(1)}, f32[128,128]{1,0:T(8,128)S(1)}) custom-call(bf16[2,64,128]{2,1,0:T(8,128)(2,1)} %raw_in.1, s32[2,2,1,2]{3,2,1,0:T(1,128)} %bitcast.12, bf16[256,32]{1,0:T(8,128)(2,1)} %bitcast.11, s32[2,32]{1,0:T(2,128)} %bitcast.13, s32[1,32]{1,0:T(1,128)} %bitcast.15, f32[2,32]{1,0:T(2,128)} %bitcast.14), custom_call_target="tpu_custom_call" | custom-call | tf_op jit(solution)/shard_map/pallas_call | solution.py:552
  28.7 0.7 %shard_map.78 = (f32[2,32]{1,0:T(2,128)}, f32[128,128]{1,0:T(8,128)}) custom-call(f32[2,32]{1,0:T(2,128)S(1)} %get-tuple-element.6.z_ref, f32[128,128]{1,0:T(8,128)S(1)} %get-tuple-element.7.res_ref), custom_call_target="tpu_custom_call" | custom-call | tf_op jit(solution)/shard_map/pallas_call | solution.py:600

commit v7 on v6

--- a/solution.py
+++ b/solution.py
@@ -48,37 +48,16 @@
     return jnp.sum(jnp.where(square, row, 0.0), axis=1, keepdims=True)
 
 
-def tile_map():
-    lane = iota((COLS, 8 * COLS), 1)
-    return jnp.where(
-        iota((COLS, 8 * COLS), 0) == (lane // COLS) * TILE + lane % TILE, 1.0, 0.0
-    ).astype(BF16)
-
-
-def place_columns(flat, col, tiles):
-    stacked = jnp.concatenate([flat[:, 0:COLS], flat[:, COLS:]], axis=0)
-    spread = mm(stacked, tiles)
-    own_group = iota((KD, COLS), 1) // TILE == iota((KD, COLS), 0) % 8
-    rows = [
-        jnp.where(
-            own_group,
-            spread[KD * (i // 8) : KD * (i // 8) + KD, (i % 8) * COLS : (i % 8 + 1) * COLS],
-            0.0,
-        )
-        for i in range(TILE)
-    ]
-    anchor = col + jnp.zeros((KD, COLS), F32)
-    offset = (iota((8, TILE, COLS), 2) - iota((8, TILE, COLS), 1)).astype(F32)
-    out = []
-    for g in range(4):
-        lhs = jnp.concatenate([r[8 * g : 8 * g + 8, :] for r in rows], axis=0).astype(BF16)
-        place = jnp.broadcast_to(anchor[8 * g : 8 * g + 8, None, :], (8, TILE, COLS))
-        onehot = jnp.where(place == offset, 1.0, 0.0).astype(BF16).reshape(COLS, COLS)
-        out.append(mm(lhs, onehot))
-    return [
-        jnp.concatenate([out[g][8 * i : 8 * i + 8, :] for g in range(4)], axis=0)
-        for i in range(TILE)
-    ]
+def place_columns(flat, col):
+    halves = [flat[:, 0:COLS].astype(F32), flat[:, COLS:].astype(F32)]
+    offset = iota((KD, COLS), 1) - (col + jnp.zeros((KD, COLS), F32)).astype(jnp.int32)
+    inside = (offset >= 0) & (offset < TILE)
+    rows = []
+    for i in range(TILE):
+        lanes = (offset + TILE * (i % 8)) & (COLS - 1)
+        taken = jnp.take_along_axis(halves[i // 8], lanes, axis=1, mode="promise_in_bounds")
+        rows.append(jnp.where(inside, taken, 0.0))
+    return rows
 
 
 def place_rows(row, tile_rows, first, count):
@@ -151,25 +130,6 @@
     def frame_at(offset):
         return lax.rem(frame + offset, n_frames)
 
-    barrier = pltpu.get_barrier_semaphore()
-
-    def greet_slab(i, carry):
-        for sign in (1, -1):
-            pl.semaphore_signal(
-                barrier,
-                1,
-                device_id={"slab": slab_at(sign * (HALO + 1 - i))},
-                device_id_type=MESH,
-            )
-        return carry
-
-    def greet_frame(i, carry):
-        pl.semaphore_signal(barrier, 1, device_id={"frames": frame_at(i)}, device_id_type=MESH)
-        return carry
-
-    lax.fori_loop(1, HALO + 1, greet_slab, 0)
-    lax.fori_loop(1, n_frames, greet_frame, 0)
-
     fetches = [
         pltpu.make_async_copy(source, target, fetched.at[i])
         for i, (source, target) in enumerate(
@@ -185,6 +145,26 @@
     ]
     for fetch in fetches:
         fetch.start()
+
+    barrier = pltpu.get_barrier_semaphore()
+
+    def greet_slab(i, carry):
+        for sign in (1, -1):
+            pl.semaphore_signal(
+                barrier,
+                1,
+                device_id={"slab": slab_at(sign * (HALO + 1 - i))},
+                device_id_type=MESH,
+            )
+        return carry
+
+    def greet_frame(i, carry):
+        pl.semaphore_signal(barrier, 1, device_id={"frames": frame_at(i)}, device_id_type=MESH)
+        return carry
+
+    lax.fori_loop(1, HALO + 1, greet_slab, 0)
+    lax.fori_loop(1, n_frames, greet_frame, 0)
+
     for fetch in fetches:
         fetch.wait()
 
@@ -231,9 +211,8 @@
     to_right.start()
 
     image[...] = jnp.zeros(image.shape, BF16)
-    tiles = tile_map()
     own_int = (own_row + jnp.zeros((KD, COLS), F32)).astype(jnp.int32)
-    for y, value in enumerate(place_rows(own_int, place_columns(flat, own_col, tiles), 0, EXT)):
+    for y, value in enumerate(place_rows(own_int, place_columns(flat, own_col), 0, EXT)):
         if value is not None:
             image[0:KD, y * COLS : (y + 1) * COLS] = value.astype(BF16)
     own = image[0:KD, :]
@@ -330,7 +309,7 @@
         info = pkt_in[side, 96:128, :].astype(F32) * keep
         smalls.append(info)
         theirs = jnp.concatenate([pkt_in[side, 32:64, :], pkt_in[side, 64:96, :]], axis=1)
-        wide = place_columns(theirs, info[:, 1:2], tiles)
+        wide = place_columns(theirs, info[:, 1:2])
         row = (info[:, 0:1] + jnp.zeros((KD, COLS), F32)).astype(jnp.int32)
         first = ROWS if side == 0 else 0
         low = 96 if side == 0 else 32

time: 29.5 us -> 29.1 us (0.986)
  Pallas kernels: 28.7 us -> 28.4 us
    pallas_call x1, Pallas kernels: 28.1 us -> 27.7 us  [shards(): pl.pallas_call(functools.partial(kernel, n_slab, n_frames), out_shape=(pl...]
where the time goes in v7:
time: 29.1 us; the launch traced here: 29 us
  Pallas kernels  28.4 us (98%)
  between operations  0.64 us (2%)
    pallas_call x1, Pallas kernels, shards(): pl.pallas_call(functools.partial(kernel, n_slab, n_frames), out_shape=(pl...  27.7 us
    pallas_call x1, Pallas kernels, shards(): pl.pallas_call(hand_on, out_shape=(jax.ShapeDtypeStruct((2, KD), F32), ja...  0.65 us

profile of v7, /device:TPU:1, one launch (start us, length us, event | category | flops | bytes accessed | tf_op | source)
XLA Modules:
  0.0 29.0 jit_solution(2243539706594322476)
XLA Ops:
  0.6 27.7 %shard_map.77 = (f32[2,32]{1,0:T(2,128)S(1)}, f32[128,128]{1,0:T(8,128)S(1)}) custom-call(bf16[2,64,128]{2,1,0:T(8,128)(2,1)} %raw_in.1, s32[2,2,1,2]{3,2,1,0:T(1,128)} %bitcast.12, bf16[256,32]{1,0:T(8,128)(2,1)} %bitcast.11, s32[2,32]{1,0:T(2,128)} %bitcast.13, s32[1,32]{1,0:T(1,128)} %bitcast.15, f32[2,32]{1,0:T(2,128)} %bitcast.14), custom_call_target="tpu_custom_call" | custom-call | tf_op jit(solution)/shard_map/pallas_call | solution.py:531
  28.3 0.7 %shard_map.78 = (f32[2,32]{1,0:T(2,128)}, f32[128,128]{1,0:T(8,128)}) custom-call(f32[2,32]{1,0:T(2,128)S(1)} %get-tuple-element.6.z_ref, f32[128,128]{1,0:T(8,128)S(1)} %get-tuple-element.7.res_ref), custom_call_target="tpu_custom_call" | custom-call | tf_op jit(solution)/shard_map/pallas_call | solution.py:579

commit v8 on v7

--- a/solution.py
+++ b/solution.py
@@ -112,6 +112,7 @@
     corr,
     band,
     square,
+    base_ref,
     e1_send,
     e1_recv,
     early_send,
@@ -267,11 +268,11 @@
             at = t * 96 + y0 + 12 + a
             picked = jnp.where(down == a, mixed[at : at + n, :], picked)
         place = iota((n, COLS), 1)
-        moved = jnp.zeros((n, COLS), F32)
-        for c in range(-3, 4):
-            turned = picked if c == 0 else pltpu.roll(picked, (-c) % COLS, 1)
-            within = (place + c >= 0) & (place + c < COLS)
-            moved = jnp.where((across == c) & within, turned, moved)
+        source = place + across.astype(jnp.int32)
+        moved = jnp.take_along_axis(
+            picked, source & (COLS - 1), axis=1, mode="promise_in_bounds"
+        )
+        moved = jnp.where((source >= 0) & (source < COLS), moved, 0.0)
         moved = moved.astype(BF16).astype(F32)
         if keep is not None:
             moved = moved * keep
@@ -296,6 +297,11 @@
         correct_own(t, 8, 24)
         correct_own(t, 32, 24)
     q_inner = mm_nt(frame_rows(16, ROWS), image[0:KD, 16 * COLS : ROWS * COLS])
+
+    for t in range(2):
+        base_ref[t : t + 1, 0:KD] = q_inner[t : t + 1, :] - jnp.sum(
+            gram_own * start[t], axis=0, keepdims=True
+        )
 
     to_left.wait()
     to_right.wait()
@@ -320,8 +326,6 @@
         for t in range(2):
             at = t * 96 + (0 if side == 0 else 80)
             rawx[at : at + 16, :] = pkt_in[side, 16 * t : 16 * t + 16, :].astype(F32) * keep
-    gram_left = mm_nt(image[96:128, 0 : 16 * COLS], image[0:KD, 0 : 16 * COLS])
-    gram_right = mm_nt(image[32:64, ROWS * COLS :], image[0:KD, ROWS * COLS :])
 
     for t in range(2):
         mix(t, 0, 12)
@@ -333,22 +337,25 @@
             down = jnp.broadcast_to(info[0:1, 8 + t : 9 + t], (RIM, COLS))
             across = jnp.broadcast_to(info[0:1, 10 + t : 11 + t], (RIM, COLS))
             correct(t, y0, RIM, down, across, valid[side])
-    q = (
-        q_inner
-        + mm_nt(frame_rows(0, 16), image[0:KD, 0 : 16 * COLS])
-        + mm_nt(frame_rows(ROWS, EXT), image[0:KD, ROWS * COLS :])
-    )
+    def edge(low, high, theirs):
+        both = jnp.concatenate([theirs, frame_rows(low, high)], axis=0)
+        out = mm_nt(both, image[0:KD, low * COLS : high * COLS])
+        return out[0:KD, :], out[KD : KD + 8, :]
+
+    gram_left, q_left = edge(0, 16, image[96:128, 0 : 16 * COLS])
+    gram_right, q_right = edge(ROWS, EXT, image[32:64, ROWS * COLS :])
+    q = base_ref[0:2, 0:KD] + q_left[0:2, :] + q_right[0:2, :]
 
     old = [start]
     for info in smalls:
         exact = info[:, 2:4] + info[:, 4:6] + info[:, 6:8]
         old.append([exact[:, t : t + 1] for t in range(2)])
-    grams = (gram_own, gram_left, gram_right)
+    grams = (gram_left, gram_right)
     late[HALO, 0:8, :] = compact(gram_left)
     late[HALO, 8:16, :] = jnp.zeros((8, COLS), F32)
     for t in range(2):
         rendered = sum(
-            jnp.sum(gram * x[t], axis=0, keepdims=True) for gram, x in zip(grams, old)
+            jnp.sum(gram * x[t], axis=0, keepdims=True) for gram, x in zip(grams, old[1:])
         )
         late[HALO, 8 + t : 9 + t, 0:KD] = q[t : t + 1, :] - rendered
     lax.fori_loop(1, HALO + 1, functools.partial(send, *late_set), 0)
@@ -556,6 +563,7 @@
             pltpu.VMEM((8 * EXT, COLS), F32),
             pltpu.VMEM((CHUNKS, 256, 256), BF16),
             pltpu.VMEM((KD, COLS), F32),
+            pltpu.VMEM((8, COLS), F32),
             dma((2,)),
             dma((2,)),
             dma,

time: 29.1 us -> 28.9 us (level)
  Pallas kernels: 28.4 us -> 28.1 us
where the time goes in v8:
time: 28.9 us; the launch traced here: 28.8 us
  Pallas kernels  28.1 us (97%)
  between operations  0.64 us (2%)
    pallas_call x1, Pallas kernels, shards(): pl.pallas_call(functools.partial(kernel, n_slab, n_frames), out_shape=(pl...  27.5 us
    pallas_call x1, Pallas kernels, shards(): pl.pallas_call(hand_on, out_shape=(jax.ShapeDtypeStruct((2, KD), F32), ja...  0.65 us

profile of v8, /device:TPU:1, one launch (start us, length us, event | category | flops | bytes accessed | tf_op | source)
XLA Modules:
  0.0 28.8 jit_solution(10247012994954166938)
XLA Ops:
  0.6 27.5 %shard_map.77 = (f32[2,32]{1,0:T(2,128)S(1)}, f32[128,128]{1,0:T(8,128)S(1)}) custom-call(bf16[2,64,128]{2,1,0:T(8,128)(2,1)} %raw_in.1, s32[2,2,1,2]{3,2,1,0:T(1,128)} %bitcast.12, bf16[256,32]{1,0:T(8,128)(2,1)} %bitcast.11, s32[2,32]{1,0:T(2,128)} %bitcast.13, s32[1,32]{1,0:T(1,128)} %bitcast.15, f32[2,32]{1,0:T(2,128)} %bitcast.14), custom_call_target="tpu_custom_call" | custom-call | tf_op jit(solution)/shard_map/pallas_call | solution.py:538
  28.1 0.7 %shard_map.78 = (f32[2,32]{1,0:T(2,128)}, f32[128,128]{1,0:T(8,128)}) custom-call(f32[2,32]{1,0:T(2,128)S(1)} %get-tuple-element.6.z_ref, f32[128,128]{1,0:T(8,128)S(1)} %get-tuple-element.7.res_ref), custom_call_target="tpu_custom_call" | custom-call | tf_op jit(solution)/shard_map/pallas_call | solution.py:587

commit v9 on v8

--- a/solution.py
+++ b/solution.py
@@ -112,6 +112,8 @@
     corr,
     band,
     square,
+    diag,
+    gain_rows_ref,
     base_ref,
     e1_send,
     e1_recv,
@@ -383,7 +385,6 @@
     own_x, left_x, right_x = (rows_of(pair) for pair in first_rows)
 
     arrived(early, early_recv)
-    arrived(late, late_recv)
 
     group8 = lanes8 // KD
 
@@ -400,42 +401,52 @@
 
     zero32 = jnp.zeros((KD, COLS), F32)
     zero8 = jnp.zeros((8, COLS), F32)
-    state, gains = [], []
-    before = zero32
+    gains = []
     for m in range(CHUNKS):
-        p_rows, gain_rows, diag, links = zero8, zero8, [], []
+        gain_rows = zero8
         for i in range(4):
             slot = 4 * m + i
             if slot < SLOTS:
                 keep = keep_of(slot)
-                rows = jnp.where(group8 == i, turned(late[slot, 8:16, :], KD * i), 0.0)
-                p_rows = p_rows + rows * keep
                 rows = jnp.where(group8 == i, turned(early[slot, 8:16, :], KD * i), 0.0)
                 gain_rows = gain_rows + rows * keep
-                diag.append(spread(early[slot, 0:8, :] * keep, i))
+                diag[m, KD * i : KD * i + KD, :] = spread(early[slot, 0:8, :] * keep, i)
             else:
-                diag.append(zero32)
+                diag[m, KD * i : KD * i + KD, :] = zero32
+        gain_rows_ref[m] = gain_rows
+
+    arrived(late, late_recv)
+
+    state = []
+    before = zero32
+    for m in range(CHUNKS):
+        gain_rows = gain_rows_ref[m]
+        gains.append(
+            [jnp.where(gain_rows[1:2, :] == float(b), gain_rows[0:1, :], 0.0) for b in range(BLOCKS)]
+        )
+        p_rows, links = zero8, []
+        for i in range(4):
+            slot = 4 * m + i
+            if slot < SLOTS:
+                rows = jnp.where(group8 == i, turned(late[slot, 8:16, :], KD * i), 0.0)
+                p_rows = p_rows + rows * keep_of(slot)
             after = slot + 1
             if after < SLOTS:
                 links.append(spread(late[after, 0:8, :] * keep_of(after), (i + 1) % 4))
             else:
                 links.append(zero32)
         state.append(p_rows)
-        gains.append(
-            [jnp.where(gain_rows[1:2, :] == float(b), gain_rows[0:1, :], 0.0) for b in range(BLOCKS)]
-        )
-        upper = jnp.concatenate(links, axis=0)
-        lower = upper.T
-        corner = lower[0:KD, :]
+        lower = jnp.concatenate(links, axis=0).T
         blocks = []
         for i in range(4):
-            value = diag[i]
+            value = diag[m, KD * i : KD * i + KD, :]
             if i < 3:
                 value = value + links[i]
             if i > 0:
                 value = value + lower[KD * i : KD * i + KD, :]
             blocks.append(value)
-        for at, value in ((0, blocks[0]), (1, blocks[1]), (2, blocks[2]), (3, blocks[3]), (4, corner), (5, zero32), (6, zero32), (7, before)):
+        blocks += [lower[0:KD, :], zero32, zero32, before]
+        for at, value in enumerate(blocks):
             hi, lo = split(value)
             band[m, at * KD : (at + 1) * KD, 0:COLS] = hi.astype(BF16)
             band[m, at * KD : (at + 1) * KD, COLS:] = lo.astype(BF16)
@@ -563,6 +574,8 @@
             pltpu.VMEM((8 * EXT, COLS), F32),
             pltpu.VMEM((CHUNKS, 256, 256), BF16),
             pltpu.VMEM((KD, COLS), F32),
+            pltpu.VMEM((CHUNKS, COLS, COLS), F32),
+            pltpu.VMEM((CHUNKS, 8, COLS), F32),
             pltpu.VMEM((8, COLS), F32),
             dma((2,)),
             dma((2,)),

time: 28.9 us -> 28.8 us (level)
  no operation moved by 1% of the time
where the time goes in v9:
time: 28.8 us; the launch traced here: 28.7 us
  Pallas kernels  28 us (97%)
  between operations  0.64 us (2%)
    pallas_call x1, Pallas kernels, shards(): pl.pallas_call(functools.partial(kernel, n_slab, n_frames), out_shape=(pl...  27.4 us
    pallas_call x1, Pallas kernels, shards(): pl.pallas_call(hand_on, out_shape=(jax.ShapeDtypeStruct((2, KD), F32), ja...  0.65 us

profile of v9, /device:TPU:1, one launch (start us, length us, event | category | flops | bytes accessed | tf_op | source)
XLA Modules:
  0.0 28.7 jit_solution(11955466127120572829)
XLA Ops:
  0.6 27.4 %shard_map.77 = (f32[2,32]{1,0:T(2,128)S(1)}, f32[128,128]{1,0:T(8,128)S(1)}) custom-call(bf16[2,64,128]{2,1,0:T(8,128)(2,1)} %raw_in.1, s32[2,2,1,2]{3,2,1,0:T(1,128)} %bitcast.12, bf16[256,32]{1,0:T(8,128)(2,1)} %bitcast.11, s32[2,32]{1,0:T(2,128)} %bitcast.13, s32[1,32]{1,0:T(1,128)} %bitcast.15, f32[2,32]{1,0:T(2,128)} %bitcast.14), custom_call_target="tpu_custom_call" | custom-call | tf_op jit(solution)/shard_map/pallas_call | solution.py:549
  28.0 0.7 %shard_map.78 = (f32[2,32]{1,0:T(2,128)}, f32[128,128]{1,0:T(8,128)}) custom-call(f32[2,32]{1,0:T(2,128)S(1)} %get-tuple-element.6.z_ref, f32[128,128]{1,0:T(8,128)S(1)} %get-tuple-element.7.res_ref), custom_call_target="tpu_custom_call" | custom-call | tf_op jit(solution)/shard_map/pallas_call | solution.py:600

commit v10 on v8

--- a/solution.py
+++ b/solution.py
@@ -441,6 +441,9 @@
             band[m, at * KD : (at + 1) * KD, COLS:] = lo.astype(BF16)
         before = links[3]
 
+    low_rows = (iota((8, COLS), 0) // 2) % 2 == 1
+    state = [p + pltpu.roll(p, 2, 0) for p in state]
+    state = [p + pltpu.roll(p, 4, 0) for p in state]
     total2 = jnp.where(lanes8 >= 96, left_x, 0.0)
     total3 = own_x + right_x
     for step in range(1, STEPS + 1):
@@ -451,21 +454,20 @@
         total3 = total3 + change[3]
         if step == STEPS:
             break
-        zero = jnp.zeros((8, COLS), F32)
+        parts = {}
+        for m, value in change.items():
+            hi, lo = split(value)
+            parts[m] = jnp.where(low_rows, lo, hi)
         for m in range(step // 4, (2 * HALO - step) // 4 + 1):
             beside = jnp.where(
                 lanes8 >= 96,
-                change.get(m - 1, zero),
-                jnp.where(lanes8 < 32, change.get(m + 1, zero), 0.0),
+                parts.get(m - 1, zero8),
+                jnp.where(lanes8 < 32, parts.get(m + 1, zero8), 0.0),
             )
-            a_hi, a_lo = split(change[m])
-            b_hi, b_lo = split(beside)
-            lhs = jnp.concatenate(
-                [jnp.concatenate([a_hi, a_lo], axis=0), jnp.concatenate([b_hi, b_lo], axis=0)],
-                axis=1,
-            ).astype(BF16)
+            lhs = jnp.concatenate([parts[m], beside], axis=1).astype(BF16)
             out = mm(lhs, band[m])
-            state[m] = state[m] - (out[0:8, 0:COLS] + out[8:16, 0:COLS] + out[0:8, COLS:])
+            both = out[:, 0:COLS] + out[:, COLS:]
+            state[m] = state[m] - (both + pltpu.roll(both, 2, 0))
 
     own_lane = lanes8 < 32
     two_rows = iota((8, COLS), 0) < 2

time: 28.9 us -> 28.9 us (level)
  no operation moved by 1% of the time
where the time goes in v10:
time: 28.9 us; the launch traced here: 28.8 us
  Pallas kernels  28.1 us (97%)
  between operations  0.64 us (2%)
    pallas_call x1, Pallas kernels, shards(): pl.pallas_call(functools.partial(kernel, n_slab, n_frames), out_shape=(pl...  27.5 us
    pallas_call x1, Pallas kernels, shards(): pl.pallas_call(hand_on, out_shape=(jax.ShapeDtypeStruct((2, KD), F32), ja...  0.65 us

profile of v10, /device:TPU:1, one launch (start us, length us, event | category | flops | bytes accessed | tf_op | source)
XLA Modules:
  0.0 28.8 jit_solution(12034574566485343492)
XLA Ops:
  0.6 27.5 %shard_map.77 = (f32[2,32]{1,0:T(2,128)S(1)}, f32[128,128]{1,0:T(8,128)S(1)}) custom-call(bf16[2,64,128]{2,1,0:T(8,128)(2,1)} %raw_in.1, s32[2,2,1,2]{3,2,1,0:T(1,128)} %bitcast.12, bf16[256,32]{1,0:T(8,128)(2,1)} %bitcast.11, s32[2,32]{1,0:T(2,128)} %bitcast.13, s32[1,32]{1,0:T(1,128)} %bitcast.15, f32[2,32]{1,0:T(2,128)} %bitcast.14), custom_call_target="tpu_custom_call" | custom-call | tf_op jit(solution)/shard_map/pallas_call | solution.py:540
  28.1 0.7 %shard_map.78 = (f32[2,32]{1,0:T(2,128)}, f32[128,128]{1,0:T(8,128)}) custom-call(f32[2,32]{1,0:T(2,128)S(1)} %get-tuple-element.6.z_ref, f32[128,128]{1,0:T(8,128)S(1)} %get-tuple-element.7.res_ref), custom_call_target="tpu_custom_call" | custom-call | tf_op jit(solution)/shard_map/pallas_call | solution.py:589
